TPU v7x, 128 devices: a whole 4x4x4 slice. The times are simulated.
128 devices in a mesh: dp: 8 (over y, z_lo), mp: 16 (over x, z_hi, core).
Axes of the slice: x: 4, y: 4, z: 4 (z_hi: 2, z_lo: 2; z = z_hi * 2 + z_lo), core: 2. Of those that a mesh axis runs over, the one named last changes fastest.
Arguments:
- tokens: bfloat16 [8192, 8192], P(('dp', 'mp')), may hold values from -6 to 6
- row_counts: int32 [8, 16], replicated, may hold values from 8 to 64, as said below
- gate_blocks: bfloat16 [64, 16, 128, 256], P('mp'), may hold values from -0.125 to 0.125
- gate_index: int32 [64, 16], P('mp'), may hold values from 0 to 63, as said below
- up_blocks: bfloat16 [64, 16, 128, 256], P('mp'), may hold values from -0.125 to 0.125
- up_index: int32 [64, 16], P('mp'), may hold values from 0 to 63, as said below
- down_blocks: bfloat16 [64, 16, 256, 128], P('mp'), may hold values from -0.09375 to 0.09375
- down_index: int32 [64, 16], P('mp'), may hold values from 0 to 63, as said below
Outputs:
- layer_out: bfloat16 [8192, 8192], P(('dp', 'mp'))
Inputs may be any that keep to these rules, and one draw needn't show every extreme that they name: `row_counts`: every entry is a multiple of 8; the entries of one column (one mp index) add up to 32 times the number of dp indices, and every column holds one entry equal to 64. `gate_index`: each row holds 16 distinct block rows in increasing order. `up_index`: each row holds 16 distinct block rows in increasing order. `down_index`: each row holds 16 distinct block columns in increasing order.
All inputs are finite; a program needn't handle non-finite values.
Results may differ from a plain program's by a relative error of at most 0.013.
Values may be sent and summed in bfloat16 or wider, within the bound.
No kernel may reach another device: no remote copies, remote signals or barrier semaphores. Data moves between devices by JAX's collectives and lax.ppermute only.
A program may use at most 192 MiB of HBM per device.

v0:
```python
import functools

import jax
import jax.numpy as jnp
from jax import lax
from jax.experimental import pallas as pl
from jax.experimental.pallas import tpu as pltpu
from jax.sharding import PartitionSpec as P


NX = 4
MP = [(x, z, c) for x in range(NX) for z in range(2) for c in range(2)]


def mp_index(x, z, c):
    return (x % NX) * 4 + (z % 2) * 2 + (c % 2)


def shift_pairs(dx, dz, dc):
    return [(mp_index(x, z, c), mp_index(x + dx, z + dz, c + dc)) for x, z, c in MP]


def shift(value, dx=0, dz=0, dc=0):
    return lax.ppermute(value, "mp", shift_pairs(dx, dz, dc))


ORDER = [(dx, dz) for dx in range(NX) for dz in range(2)]


def gather_z_first(part):
    cross = shift(part, dz=1)
    pair = jnp.concatenate([part, cross], axis=0)
    left = shift(pair, dx=1)
    right = shift(pair, dx=-1)
    far = shift(pair, dx=2)
    return [(pair, [(0, 0), (0, 1)]), (left, [(3, 0), (3, 1)]), (right, [(1, 0), (1, 1)]), (far, [(2, 0), (2, 1)])]


def gather_x_first(part):
    left = shift(part, dx=1)
    right = shift(part, dx=-1)
    far = shift(part, dx=2)
    cross = shift(part, dz=1)
    three = jnp.concatenate([left, right, far], axis=0)
    three_cross = shift(three, dz=1)
    return [(part, [(0, 0)]), (three, [(3, 0), (1, 0), (2, 0)]),
            (cross, [(0, 1)]), (three_cross, [(3, 1), (1, 1), (2, 1)])]


Z_LAST = [[(2, 0)], [(2, 1)], [(1, 0), (1, 1)], [(3, 0), (3, 1)], [(0, 0), (0, 1)]]
Z_LAST_DIRECT = [[(dx, 0), (dx, 1)] for dx in (2, 1, 3, 0)]
Z_FIRST = [[(dx, 1) for dx in range(NX)], [(dx, 0) for dx in range(NX)]]


def layer_kernel(loads, stores, nonzero, own_columns,
                 gate_index, up_index, down_index,
                 gate_own, gate_other, up_own, up_other, down_own, down_other, *rest):
    n_in, n_out = 1 + max(p[0] for p in loads), 1 + max(p[0] for p in stores)
    pieces, outs = rest[:n_in], rest[n_in:n_in + n_out]
    x_all, gate_left, up_left, total = rest[n_in + n_out:]
    step = pl.program_id(0)
    block_width = gate_own.shape[2]
    unit_width = gate_own.shape[3]

    @pl.when(step == 0)
    def _():
        for which, piece_row, rows, row, column, width in loads:
            x_all[row:row + rows, column:column + width] = pieces[which][piece_row:piece_row + rows, :]
        total[...] = jnp.zeros_like(total)

    def run(gate_ref, up_ref, down_ref):
        def project(index, weights, left):
            for k in range(nonzero):
                at = pl.multiple_of(index[step, k] * block_width, block_width)
                left[:, k * block_width:(k + 1) * block_width] = x_all[:, pl.ds(at, block_width)]
            return jnp.dot(left[...], weights[0].reshape(nonzero * block_width, unit_width),
                           preferred_element_type=jnp.float32)

        gate = project(gate_index, gate_ref, gate_left)
        up = project(up_index, up_ref, up_left)
        hidden = (gate / (1.0 + jnp.exp(-gate)) * up).astype(jnp.bfloat16)
        for k in range(0, nonzero, 2):
            pair = jnp.concatenate([down_ref[0, k], down_ref[0, k + 1]], axis=1)
            value = jnp.dot(hidden, pair, preferred_element_type=jnp.float32)
            for i in range(2):
                at = pl.multiple_of(down_index[step, k + i] * block_width, block_width)
                total[:, pl.ds(at, block_width)] += value[:, i * block_width:(i + 1) * block_width]

    @pl.when(step < own_columns)
    def _():
        run(gate_own, up_own, down_own)

    @pl.when(step >= own_columns)
    def _():
        run(gate_other, up_other, down_other)

    @pl.when(step == 2 * own_columns - 1)
    def _():
        for which, out_row, rows, row, column, width in stores:
            outs[which][out_row:out_row + rows, :] = total[row:row + rows, column:column + width].astype(jnp.bfloat16)


def run_layer(gathered_parts, sent_parts, width, index_own, index_other, weights_own, weights_other):
    loads, stores, pieces, out_shapes, all_rows = [], [], [], [], 0
    for gathered, rows, row, column in gathered_parts:
        all_rows = max(all_rows, row + 8 * rows)
        for array, keys in gathered:
            for i, key in enumerate(keys):
                loads.append((len(pieces), i * rows, rows, row + ORDER.index(key) * rows, column, array.shape[1]))
            pieces.append(array)
    for sends, rows, row, column, part_width in sent_parts:
        for keys in sends:
            for i, key in enumerate(keys):
                stores.append((len(out_shapes), i * rows, rows, row + ORDER.index(key) * rows, column, part_width))
            out_shapes.append((len(keys) * rows, part_width))
    own_columns, nonzero, block_width, _ = weights_own[0].shape
    tables = [jnp.concatenate([a, b], axis=0) for a, b in zip(index_own, index_other)]

    def own_map(j, *_):
        return (jnp.minimum(j, own_columns - 1), 0, 0, 0)

    def other_map(j, *_):
        return (jnp.maximum(j - own_columns, 0), 0, 0, 0)

    weight_specs, weights = [], []
    for own, other in zip(weights_own, weights_other):
        shape = (1,) + own.shape[1:]
        weight_specs += [pl.BlockSpec(shape, own_map), pl.BlockSpec(shape, other_map)]
        weights += [own, other]
    sums = pl.pallas_call(
        functools.partial(layer_kernel, loads, stores, nonzero, own_columns),
        grid_spec=pltpu.PrefetchScalarGridSpec(
            num_scalar_prefetch=3,
            grid=(2 * own_columns,),
            in_specs=weight_specs + [pl.BlockSpec(memory_space=pltpu.VMEM)] * len(pieces),
            out_specs=[pl.BlockSpec(memory_space=pltpu.VMEM)] * len(out_shapes),
            scratch_shapes=[
                pltpu.VMEM((all_rows, width), jnp.bfloat16),
                pltpu.VMEM((all_rows, nonzero * block_width), jnp.bfloat16),
                pltpu.VMEM((all_rows, nonzero * block_width), jnp.bfloat16),
                pltpu.VMEM((all_rows, width), jnp.float32),
            ],
        ),
        out_shape=[jax.ShapeDtypeStruct(s, jnp.bfloat16) for s in out_shapes],
        compiler_params=pltpu.CompilerParams(
            dimension_semantics=("arbitrary",), vmem_limit_bytes=45 * 1024 * 1024),
        name="sparse_ffn",
    )(*tables, *weights, *pieces)
    split, at = [], 0
    for sends, *_ in sent_parts:
        split.append(sums[at:at + len(sends)])
        at += len(sends)
    return split


def wide(value):
    return value.astype(jnp.float32)


def narrow(value):
    return value.astype(jnp.bfloat16)


def scatter_z_last(sums):
    far_0, far_1, next_1, next_3, own = sums
    rows = far_0.shape[0]
    got_0 = shift(far_0, dx=1)
    got_1 = shift(far_1, dx=-1)
    to_1 = jnp.concatenate([narrow(wide(next_1[:rows]) + wide(got_0)), next_1[rows:]], axis=0)
    to_3 = jnp.concatenate([next_3[:rows], narrow(wide(next_3[rows:]) + wide(got_1))], axis=0)
    got_left = shift(to_1, dx=1)
    got_right = shift(to_3, dx=-1)
    met = wide(own) + wide(got_left) + wide(got_right)
    got_z = shift(narrow(met[rows:]), dz=1)
    return narrow(met[:rows] + wide(got_z))


def scatter_z_last_direct(sums):
    far, next_1, next_3, own = sums
    rows = far.shape[0] // 2
    got = [shift(far, dx=2), shift(next_1, dx=1), shift(next_3, dx=-1)]
    met = wide(own) + wide(got[0]) + wide(got[1]) + wide(got[2])
    got_z = shift(narrow(met[rows:]), dz=1)
    return narrow(met[:rows] + wide(got_z))


def scatter_z_first(sums):
    cross_1, cross_0 = sums
    rows = cross_1.shape[0] // NX
    got_cross = shift(cross_1, dz=1)
    met = [wide(cross_0[i * rows:(i + 1) * rows]) + wide(got_cross[i * rows:(i + 1) * rows]) for i in range(NX)]
    return narrow(met[0] + wide(shift(narrow(met[1]), dx=1))
                  + wide(shift(narrow(met[3]), dx=-1))
                  + wide(shift(narrow(met[2]), dx=2)))


UNIT = 8


def copy_units(sources, index, out_widths, head=None, count=None):
    units = index.shape[0]
    in_starts = [sum(s.shape[1] for s in sources[:i]) for i in range(len(sources))]
    out_starts = [sum(out_widths[:i]) for i in range(len(out_widths))]
    spans = []
    for i, source in enumerate(sources):
        for o, width in enumerate(out_widths):
            low = max(in_starts[i], out_starts[o])
            high = min(in_starts[i] + source.shape[1], out_starts[o] + width)
            if low < high:
                spans.append((i, low - in_starts[i], o, low - out_starts[o], high - low))
    ins_all = list(sources) if head is None else [*sources, head]
    table = index if head is None else jnp.concatenate([index, count[None]])

    def kernel(table, *refs):
        ins, outs = refs[:len(sources)], refs[len(ins_all):]
        for unit in range(units):
            start = pl.multiple_of(table[unit] * UNIT, UNIT)
            for i, from_column, o, to_column, width in spans:
                if head is not None and unit == 0:
                    value = refs[len(sources)][...]
                else:
                    value = ins[i][pl.ds(start, UNIT), from_column:from_column + width]
                    if head is not None:
                        value = jnp.where(unit < table[units], value, jnp.zeros_like(value))
                outs[o][unit * UNIT:(unit + 1) * UNIT, to_column:to_column + width] = value

    return pl.pallas_call(
        kernel,
        in_specs=[pl.BlockSpec(memory_space=pltpu.SMEM)] + [pl.BlockSpec(memory_space=pltpu.VMEM)] * len(ins_all),
        out_specs=[pl.BlockSpec(memory_space=pltpu.VMEM)] * len(out_widths),
        out_shape=[jax.ShapeDtypeStruct((units * UNIT, w), jnp.bfloat16) for w in out_widths],
        compiler_params=pltpu.CompilerParams(vmem_limit_bytes=8 * 1024 * 1024),
        name="copy_units",
    )(table, *ins_all)


def plan(row_counts, own_dp, own_mp):
    n_dp = row_counts.shape[0]
    counts = lax.dynamic_slice_in_dim(row_counts, own_mp, 1, axis=1)[:, 0] // UNIT - 1
    ends = jnp.cumsum(counts)
    firsts = ends - counts
    ids = jnp.arange(n_dp, dtype=jnp.int32)
    own_first = lax.dynamic_index_in_dim(firsts, own_dp, keepdims=False)
    own_count = lax.dynamic_index_in_dim(counts, own_dp, keepdims=False)
    return n_dp, firsts, ends, ids, own_first, own_count


def run(tokens, row_counts, gate_blocks, gate_index, up_blocks, up_index, down_blocks, down_index):
    own_dp = lax.axis_index("dp")
    own_mp = lax.axis_index("mp")
    rows, width = tokens.shape
    block_width = gate_blocks.shape[2]
    width_p = (width // block_width * 7 // 16) * block_width
    width_sp = (width // block_width * 8 // 16) * block_width
    n_dp, firsts, ends, ids, own_first, own_count = plan(row_counts, own_dp, own_mp)
    units = rows // UNIT
    kept_units = units // 2 - 1
    numbers = jnp.arange(kept_units, dtype=jnp.int32) * n_dp + own_dp
    source_of = jnp.sum((ends[None, :] <= numbers[:, None]).astype(jnp.int32), axis=1)
    back = jnp.clip((firsts + (own_dp - firsts) % n_dp) // n_dp, 0, kept_units - 1)
    send = jnp.minimum((ids - own_first) % n_dp + 1, units - 1)
    restore = (own_first + jnp.arange(units, dtype=jnp.int32) - 1) % n_dp
    index_own = (gate_index, up_index, down_index)
    index_both = shift(jnp.stack(index_own), dc=1)
    index_other = (index_both[0], index_both[1], index_both[2])
    weights_own = (gate_blocks, up_blocks, down_blocks)
    weights_other = tuple(shift(w, dc=1) for w in weights_own)
    still = gather_z_first(tokens[:UNIT])
    rolled, = copy_units([tokens], send, [width])
    spread = lax.all_to_all(rolled, "dp", split_axis=0, concat_axis=0, tiled=True)
    kept = kept_units * UNIT
    part_p, part_q = copy_units([spread], source_of, [width_p, width - width_p])
    gathered_parts = [
        (gather_z_first(part_p), kept, 0, 0), (gather_x_first(part_q), kept, 0, width_p), (still, UNIT, 8 * kept, 0)
    ]
    sent_parts = [
        (Z_LAST, kept, 0, 0, width_sp),
        (Z_FIRST, kept, 0, width_sp, width - width_sp),
        (Z_LAST_DIRECT, UNIT, 8 * kept, 0, width),
    ]
    sums_p, sums_q, sums_still = run_layer(
        gathered_parts, sent_parts, width, index_own, index_other, weights_own, weights_other)
    part_p = scatter_z_last(sums_p)
    part_q = scatter_z_first(sums_q)
    returned, = copy_units([part_p, part_q], back, [width])
    received = lax.all_to_all(returned, "dp", split_axis=0, concat_axis=0, tiled=True)
    still = scatter_z_last_direct(sums_still)
    restored, = copy_units([received], restore, [width], still, own_count + 1)
    return restored


def solution(mesh):
    in_specs = (
        P(("dp", "mp"), None),
        P(),
        P("mp", None, None, None),
        P("mp", None),
        P("mp", None, None, None),
        P("mp", None),
        P("mp", None, None, None),
        P("mp", None),
    )
    out_specs = P(("dp", "mp"), None)
    return jax.shard_map(run, mesh=mesh, in_specs=in_specs, out_specs=out_specs, check_vma=False)
```

profile of v0, /device:TPU:0, one launch (start us, length us, event | category | flops | bytes accessed | tf_op | source)
XLA Modules:
  0.0 168.8 jit_solution(17023957351950195731)
XLA Ops:
  0.0 0.8 pad_add_fusion
  0.8 0.9 slice.65
  1.7 4.1 %collective-permute-start.13 = (bf16[8,8192]{1,0:T(8,128)(2,1)S(1)}, bf16[8,8192]{1,0:T(8,128)(2,1)S(1)}, u32[]{:S(2)}, u32[]{:S(2)}) collective-permute-start(bf16[8,8192]{1,0:T(8,128)(2,1)S(1)} %slice.65), channel_id=1, source_target_pairs={{0,2},{1,3},{2,0},{3,1},{4,6},{5,7},{6,4},{7,5},{8,10},{9,11},{10,... | collective-permute-start | bytes 393224 | tf_op jit(solution)/shard_map/ppermute | solution.py:24
  5.8 0.9 dynamic-slice_reduce_fusion
  7.4 0.6 fusion.7.table
  8.1 1.2 copy-done
  9.3 1.6 copy_units.4
  10.8 4.9 %all-to-all-start = ((bf16[8,8,8192]{2,1,0:T(8,128)(2,1)}), bf16[8,8,8192]{2,1,0:T(8,128)(2,1)S(1)}, u32[]{:S(2)}, u32[]{:S(2)}) async-start(bf16[8,8,8192]{2,1,0:T(8,128)(2,1)} %bitcast.7), calls=%async_computation | async-start | bytes 2097152 | tf_op jit(solution)/shard_map/all_to_all | solution.py:270
  16.6 3.1 %collective-permute-start.16 = (bf16[16,8192]{1,0:T(8,128)(2,1)S(1)}, bf16[16,8192]{1,0:T(8,128)(2,1)S(1)}, u32[]{:S(2)}, u32[]{:S(2)}) collective-permute-start(bf16[16,8192]{1,0:T(8,128)(2,1)S(1)} %pad_maximum_fusion.2.rest_8_), channel_id=1, source_target_pairs={{0,8},{1,9},{2,10},{3,11},{4,12},{5,13},{6,14},{7,15},{8,0},{9,1},... | collective-permute-start | bytes 786440 | tf_op jit(solution)/shard_map/ppermute | solution.py:24
  19.7 12.7 %all-to-all-done = bf16[8,8,8192]{2,1,0:T(8,128)(2,1)S(1)} async-done(((bf16[8,8,8192]{2,1,0:T(8,128)(2,1)}), bf16[8,8,8192]{2,1,0:T(8,128)(2,1)S(1)}, u32[]{:S(2)}, u32[]{:S(2)}) %all-to-all-start) | async-done | bytes 1048608 | tf_op jit(solution)/shard_map/all_to_all | solution.py:270
  33.0 1.2 collective-permute-start.4
  34.3 2.8 %collective-permute-start.15 = (bf16[16,8192]{1,0:T(8,128)(2,1)S(1)}, bf16[16,8192]{1,0:T(8,128)(2,1)S(1)}, u32[]{:S(2)}, u32[]{:S(2)}) collective-permute-start(bf16[16,8192]{1,0:T(8,128)(2,1)S(1)} %pad_maximum_fusion.2.rest_8_), channel_id=1, source_target_pairs={{0,12},{1,13},{2,14},{3,15},{4,0},{5,1},{6,2},{7,3},{8,4},{9,5},{1... | collective-permute-start | bytes 786440 | tf_op jit(solution)/shard_map/ppermute | solution.py:24
  37.1 2.9 %collective-permute-done.4 = bf16[24,3584]{1,0:T(8,128)(2,1)S(1)} collective-permute-done((bf16[24,3584]{1,0:T(8,128)(2,1)S(1)}, bf16[24,3584]{1,0:T(8,128)(2,1)S(1)}, u32[]{:S(2)}, u32[]{:S(2)}) %collective-permute-start.4) | collective-permute-done | bytes 172064 | tf_op jit(solution)/shard_map/ppermute | solution.py:24
  40.0 1.5 collective-permute-start.8
  41.7 1.4 collective-permute-start.14
  43.1 6.3 %collective-permute-done.8 = bf16[24,4608]{1,0:T(8,128)(2,1)S(1)} collective-permute-done((bf16[24,4608]{1,0:T(8,128)(2,1)S(1)}, bf16[24,4608]{1,0:T(8,128)(2,1)S(1)}, u32[]{:S(2)}, u32[]{:S(2)}) %collective-permute-start.8) | collective-permute-done | bytes 221216 | tf_op jit(solution)/shard_map/ppermute | solution.py:24
  49.4 1.7 %collective-permute-start.9 = (bf16[24,4608]{1,0:T(8,128)(2,1)S(1)}, bf16[24,4608]{1,0:T(8,128)(2,1)S(1)}, u32[]{:S(2)}, u32[]{:S(2)}) collective-permute-start(bf16[24,4608]{1,0:T(8,128)(2,1)S(1)} %get-tuple-element.19.rest_4_), channel_id=1, source_target_pairs={{0,12},{1,13},{2,14},{3,15},{4,0},{5,1},{6,2},{7,3},{8,4},{9,5},{1... | collective-permute-start | bytes 663560 | tf_op jit(solution)/shard_map/ppermute | solution.py:24
  51.1 1.1 collective-permute-done.14.rest_9_
  52.2 1.7 %collective-permute-start.11 = (bf16[24,4608]{1,0:T(8,128)(2,1)S(1)}, bf16[24,4608]{1,0:T(8,128)(2,1)S(1)}, u32[]{:S(2)}, u32[]{:S(2)}) collective-permute-start(bf16[24,4608]{1,0:T(8,128)(2,1)S(1)} %get-tuple-element.19.rest_4_), channel_id=1, source_target_pairs={{0,2},{1,3},{2,0},{3,1},{4,6},{5,7},{6,4},{7,5},{8,10},{9,11},{10,... | collective-permute-start | bytes 663560 | tf_op jit(solution)/shard_map/ppermute | solution.py:24
  54.0 1.5 collective-permute-done.9
  55.5 2.6 %collective-permute-start.10 = (bf16[24,4608]{1,0:T(8,128)(2,1)S(1)}, bf16[24,4608]{1,0:T(8,128)(2,1)S(1)}, u32[]{:S(2)}, u32[]{:S(2)}) collective-permute-start(bf16[24,4608]{1,0:T(8,128)(2,1)S(1)} %get-tuple-element.19.rest_4_), channel_id=1, source_target_pairs={{0,8},{1,9},{2,10},{3,11},{4,12},{5,13},{6,14},{7,15},{8,0},{9,1},... | collective-permute-start | bytes 663560 | tf_op jit(solution)/shard_map/ppermute | solution.py:24
  58.1 1.5 collective-permute-done.11.rest_6_
  59.6 1.8 %collective-permute-start.7 = (bf16[48,3584]{1,0:T(8,128)(2,1)S(1)}, bf16[48,3584]{1,0:T(8,128)(2,1)S(1)}, u32[]{:S(2)}, u32[]{:S(2)}) collective-permute-start(bf16[48,3584]{1,0:T(8,128)(2,1)S(1)} %constant_dynamic-update-slice_fusion.rest_0_), channel_id=1, source_target_pairs={{0,8},{1,9},{2,10},{3,11},{4,12},{5,13},{6,14},{7,15},{8,0},{9,1},... | collective-permute-start | bytes 1032200 | tf_op jit(solution)/shard_map/ppermute | solution.py:24
  61.4 3.8 %collective-permute-done.10 = bf16[24,4608]{1,0:T(8,128)(2,1)S(1)} collective-permute-done((bf16[24,4608]{1,0:T(8,128)(2,1)S(1)}, bf16[24,4608]{1,0:T(8,128)(2,1)S(1)}, u32[]{:S(2)}, u32[]{:S(2)}) %collective-permute-start.10) | collective-permute-done | bytes 221216 | tf_op jit(solution)/shard_map/ppermute | solution.py:24
  65.3 5.1 %collective-permute-start.6 = (bf16[48,3584]{1,0:T(8,128)(2,1)S(1)}, bf16[48,3584]{1,0:T(8,128)(2,1)S(1)}, u32[]{:S(2)}, u32[]{:S(2)}) collective-permute-start(bf16[48,3584]{1,0:T(8,128)(2,1)S(1)} %constant_dynamic-update-slice_fusion.rest_0_), channel_id=1, source_target_pairs={{0,12},{1,13},{2,14},{3,15},{4,0},{5,1},{6,2},{7,3},{8,4},{9,5},{1... | collective-permute-start | bytes 1032200 | tf_op jit(solution)/shard_map/ppermute | solution.py:24
  72.1 4.1 %collective-permute-done.6.rest_2_ = bf16[48,3584]{1,0:T(8,128)(2,1)S(1)} collective-permute-done((bf16[48,3584]{1,0:T(8,128)(2,1)S(1)}, bf16[48,3584]{1,0:T(8,128)(2,1)S(1)}, u32[]{:S(2)}, u32[]{:S(2)}) %collective-permute-start.6) | collective-permute-done | bytes 344096 | tf_op jit(solution)/shard_map/ppermute | solution.py:24
  76.1 0.9 collective-permute-start.5
  77.1 7.5 %collective-permute-done.5.rest_1_ = bf16[48,3584]{1,0:T(8,128)(2,1)S(1)} collective-permute-done((bf16[48,3584]{1,0:T(8,128)(2,1)S(1)}, bf16[48,3584]{1,0:T(8,128)(2,1)S(1)}, u32[]{:S(2)}, u32[]{:S(2)}) %collective-permute-start.5) | collective-permute-done | bytes 344096 | tf_op jit(solution)/shard_map/ppermute | solution.py:24
  84.8 18.9 %sparse_ffn.1 = (bf16[24,4096]{1,0:T(8,128)(2,1)S(1)}, bf16[24,4096]{1,0:T(8,128)(2,1)S(1)}, bf16[48,4096]{1,0:T(8,128)(2,1)S(1)}, bf16[48,4096]{1,0:T(8,128)(2,...) custom-call(s32[8,16]{1,0:T(8,128)S(1)} %get-tuple-element.42.gate_i, ...), custom_call_target="tpu_custom_call" | custom-call | tf_op jit(solution)/shard_map/sparse_ffn/pallas_call | solution.py:130
  103.7 2.6 %collective-permute-start.19 = (bf16[24,4096]{1,0:T(8,128)(2,1)S(1)}, bf16[24,4096]{1,0:T(8,128)(2,1)S(1)}, u32[]{:S(2)}, u32[]{:S(2)}) collective-permute-start(bf16[24,4096]{1,0:T(8,128)(2,1)S(1)} %get-tuple-element.24), channel_id=1, source_target_pairs={{0,12},{1,13},{2,14},{3,15},{4,0},{5,1},{6,2},{7,3},{8,4},{9,5},{1... | collective-permute-start | bytes 589832 | tf_op jit(solution)/shard_map/ppermute | solution.py:24
  106.3 0.6 and_select_fusion.3
  107.1 1.5 collective-permute-start.26
  108.6 2.6 %collective-permute-start.27 = (bf16[16,8192]{1,0:T(8,128)(2,1)S(1)}, bf16[16,8192]{1,0:T(8,128)(2,1)S(1)}, u32[]{:S(2)}, u32[]{:S(2)}) collective-permute-start(bf16[16,8192]{1,0:T(8,128)(2,1)S(1)} %get-tuple-element.29), channel_id=1, source_target_pairs={{0,4},{1,5},{2,6},{3,7},{4,8},{5,9},{6,10},{7,11},{8,12},{9,13},{1... | collective-permute-start | bytes 786440 | tf_op jit(solution)/shard_map/ppermute | solution.py:24
  111.2 0.6 collective-permute-start.28
  111.8 4.0 %collective-permute-start.22 = (bf16[96,4096]{1,0:T(8,128)(2,1)S(1)}, bf16[96,4096]{1,0:T(8,128)(2,1)S(1)}, u32[]{:S(2)}, u32[]{:S(2)}) collective-permute-start(bf16[96,4096]{1,0:T(8,128)(2,1)S(1)} %get-tuple-element.26), channel_id=1, source_target_pairs={{0,2},{1,3},{2,0},{3,1},{4,6},{5,7},{6,4},{7,5},{8,10},{9,11},{10,... | collective-permute-start | bytes 2359304 | tf_op jit(solution)/shard_map/ppermute | solution.py:24
  115.9 1.3 collective-permute-done.17
  117.2 3.0 %collective-permute-start.20 = (bf16[48,4096]{1,0:T(8,128)(2,1)S(1)}, bf16[48,4096]{1,0:T(8,128)(2,1)S(1)}, u32[]{:S(2)}, u32[]{:S(2)}) collective-permute-start(bf16[48,4096]{1,0:T(8,128)(2,1)S(1)} %pad_maximum_fusion.1), channel_id=1, source_target_pairs={{0,12},{1,13},{2,14},{3,15},{4,0},{5,1},{6,2},{7,3},{8,4},{9,5},{1... | collective-permute-start | bytes 1179656 | tf_op jit(solution)/shard_map/ppermute | solution.py:24
  120.4 2.3 %collective-permute-done.27 = bf16[16,8192]{1,0:T(8,128)(2,1)S(1)} collective-permute-done((bf16[16,8192]{1,0:T(8,128)(2,1)S(1)}, bf16[16,8192]{1,0:T(8,128)(2,1)S(1)}, u32[]{:S(2)}, u32[]{:S(2)}) %collective-permute-start.27) | collective-permute-done | bytes 262176 | tf_op jit(solution)/shard_map/ppermute | solution.py:24
  122.8 6.8 %collective-permute-start.29 = (bf16[8,8192]{1,0:T(8,128)(2,1)S(1)}, bf16[8,8192]{1,0:T(8,128)(2,1)S(1)}, u32[]{:S(2)}, u32[]{:S(2)}) collective-permute-start(bf16[8,8192]{1,0:T(8,128)(2,1)S(1)} %slice.115), channel_id=1, source_target_pairs={{0,2},{1,3},{2,0},{3,1},{4,6},{5,7},{6,4},{7,5},{8,10},{9,11},{10,... | collective-permute-start | bytes 393224 | tf_op jit(solution)/shard_map/ppermute | solution.py:24
  129.8 6.8 %collective-permute-start.21 = (bf16[24,4096]{1,0:T(8,128)(2,1)S(1)}, bf16[24,4096]{1,0:T(8,128)(2,1)S(1)}, u32[]{:S(2)}, u32[]{:S(2)}) collective-permute-start(bf16[24,4096]{1,0:T(8,128)(2,1)S(1)} %slice.114), channel_id=1, source_target_pairs={{0,2},{1,3},{2,0},{3,1},{4,6},{5,7},{6,4},{7,5},{8,10},{9,11},{10,... | collective-permute-start | bytes 589832 | tf_op jit(solution)/shard_map/ppermute | solution.py:24
  136.8 1.1 collective-permute-start.25
  137.8 2.2 %collective-permute-start.24 = (bf16[24,4096]{1,0:T(8,128)(2,1)S(1)}, bf16[24,4096]{1,0:T(8,128)(2,1)S(1)}, u32[]{:S(2)}, u32[]{:S(2)}) collective-permute-start(bf16[24,4096]{1,0:T(8,128)(2,1)S(1)} %get-tuple-element.36), channel_id=1, source_target_pairs={{0,12},{1,13},{2,14},{3,15},{4,0},{5,1},{6,2},{7,3},{8,4},{9,5},{1... | collective-permute-start | bytes 589832 | tf_op jit(solution)/shard_map/ppermute | solution.py:24
  140.2 7.1 %collective-permute-done.23 = bf16[24,4096]{1,0:T(8,128)(2,1)S(1)} collective-permute-done((bf16[24,4096]{1,0:T(8,128)(2,1)S(1)}, bf16[24,4096]{1,0:T(8,128)(2,1)S(1)}, u32[]{:S(2)}, u32[]{:S(2)}) %collective-permute-start.23) | collective-permute-done | bytes 196640 | tf_op jit(solution)/shard_map/ppermute | solution.py:24
  147.3 0.6 collective-permute-done.24
  148.1 1.6 copy_units.6
  149.6 3.7 %all-to-all-start.1 = ((bf16[8,8,8192]{2,1,0:T(8,128)(2,1)}), bf16[8,8,8192]{2,1,0:T(8,128)(2,1)S(1)}, u32[]{:S(2)}, u32[]{:S(2)}) async-start(bf16[8,8,8192]{2,1,0:T(8,128)(2,1)} %bitcast.9), calls=%async_computation.1 | async-start | bytes 2097152 | tf_op jit(solution)/shard_map/all_to_all | solution.py:286
  153.4 13.8 %all-to-all-done.1 = bf16[8,8,8192]{2,1,0:T(8,128)(2,1)S(1)} async-done(((bf16[8,8,8192]{2,1,0:T(8,128)(2,1)}), bf16[8,8,8192]{2,1,0:T(8,128)(2,1)S(1)}, u32[]{:S(2)}, u32[]{:S(2)}) %all-to-all-start.1) | async-done | bytes 1048608 | tf_op jit(solution)/shard_map/all_to_all | solution.py:286
  167.2 1.6 copy_units.7
  (65 shorter events, 4.9 us)
Async XLA Ops:
  0.0 77.1 %copy-start.3 = (s32[4,16]{1,0:T(4,128)S(1)}, s32[4,16]{1,0:T(4,128)}, u32[]{:S(2)}) copy-start(s32[4,16]{1,0:T(4,128)} %param.11) | copy-start | bytes 772
  0.0 77.1 %copy-start.2 = (s32[4,16]{1,0:T(4,128)S(1)}, s32[4,16]{1,0:T(4,128)}, u32[]{:S(2)}) copy-start(s32[4,16]{1,0:T(4,128)} %param.13) | copy-start | bytes 772
  0.0 77.1 %copy-start.1 = (s32[4,16]{1,0:T(4,128)S(1)}, s32[4,16]{1,0:T(4,128)}, u32[]{:S(2)}) copy-start(s32[4,16]{1,0:T(4,128)} %param.15) | copy-start | bytes 772
  0.8 32.3 %collective-permute-start = (s32[3,4,16]{2,1,0:T(4,128)S(1)}, s32[3,4,16]{2,1,0:T(4,128)S(1)}, u32[]{:S(2)}, u32[]{:S(2)}) collective-permute-start(s32[3,4,16]{2,1,0:T(4,128)S(1)} %pad_add_fusion), channel_id=1, source_target_pairs={{0,1},{1,0},{2,3},{3,2},{4,5},{5,4},{6,7},{7,6},{8,9},{9,8},{10,11... | collective-permute-start | bytes 2312 | tf_op jit(solution)/shard_map/ppermute | solution.py:24
  1.7 14.9 %collective-permute-start.13 = (bf16[8,8192]{1,0:T(8,128)(2,1)S(1)}, bf16[8,8192]{1,0:T(8,128)(2,1)S(1)}, u32[]{:S(2)}, u32[]{:S(2)}) collective-permute-start(bf16[8,8192]{1,0:T(8,128)(2,1)S(1)} %slice.65), channel_id=1, source_target_pairs={{0,2},{1,3},{2,0},{3,1},{4,6},{5,7},{6,4},{7,5},{8,10},{9,11},{10,... | collective-permute-start | bytes 393224 | tf_op jit(solution)/shard_map/ppermute | solution.py:24
  8.0 1.2 copy-start
  10.8 21.6 %all-to-all-start = ((bf16[8,8,8192]{2,1,0:T(8,128)(2,1)}), bf16[8,8,8192]{2,1,0:T(8,128)(2,1)S(1)}, u32[]{:S(2)}, u32[]{:S(2)}) async-start(bf16[8,8,8192]{2,1,0:T(8,128)(2,1)} %bitcast.7), calls=%async_computation | async-start | bytes 2097152 | tf_op jit(solution)/shard_map/all_to_all | solution.py:270
  15.8 69.0 %collective-permute-start.1 = (bf16[4,16,128,256]{3,2,1,0:T(8,128)(2,1)}, bf16[4,16,128,256]{3,2,1,0:T(8,128)(2,1)}, u32[]{:S(2)}, u32[]{:S(2)}) collective-permute-start(bf16[4,16,128,256]{3,2,1,0:T(8,128)(2,1)} %gate_own.1), channel_id=1, source_target_pairs={{0,1},{1,0},{2,3},{3,2},{4,5},{5,4},{6,7},{7,6},{8,9},{9,8},{10,11... | collective-permute-start | bytes 12582920 | tf_op jit(solution)/shard_map/ppermute | solution.py:24
  15.8 69.0 %collective-permute-start.2 = (bf16[4,16,128,256]{3,2,1,0:T(8,128)(2,1)}, bf16[4,16,128,256]{3,2,1,0:T(8,128)(2,1)}, u32[]{:S(2)}, u32[]{:S(2)}) collective-permute-start(bf16[4,16,128,256]{3,2,1,0:T(8,128)(2,1)} %up_own.1), channel_id=1, source_target_pairs={{0,1},{1,0},{2,3},{3,2},{4,5},{5,4},{6,7},{7,6},{8,9},{9,8},{10,11... | collective-permute-start | bytes 12582920 | tf_op jit(solution)/shard_map/ppermute | solution.py:24
  16.3 68.5 %collective-permute-start.3 = (bf16[4,16,256,128]{3,2,1,0:T(8,128)(2,1)}, bf16[4,16,256,128]{3,2,1,0:T(8,128)(2,1)}, u32[]{:S(2)}, u32[]{:S(2)}) collective-permute-start(bf16[4,16,256,128]{3,2,1,0:T(8,128)(2,1)} %down_own.1), channel_id=1, source_target_pairs={{0,1},{1,0},{2,3},{3,2},{4,5},{5,4},{6,7},{7,6},{8,9},{9,8},{10,11... | collective-permute-start | bytes 12582920 | tf_op jit(solution)/shard_map/ppermute | solution.py:24
  16.6 17.7 %collective-permute-start.16 = (bf16[16,8192]{1,0:T(8,128)(2,1)S(1)}, bf16[16,8192]{1,0:T(8,128)(2,1)S(1)}, u32[]{:S(2)}, u32[]{:S(2)}) collective-permute-start(bf16[16,8192]{1,0:T(8,128)(2,1)S(1)} %pad_maximum_fusion.2.rest_8_), channel_id=1, source_target_pairs={{0,8},{1,9},{2,10},{3,11},{4,12},{5,13},{6,14},{7,15},{8,0},{9,1},... | collective-permute-start | bytes 786440 | tf_op jit(solution)/shard_map/ppermute | solution.py:24
  33.0 7.0 %collective-permute-start.4 = (bf16[24,3584]{1,0:T(8,128)(2,1)S(1)}, bf16[24,3584]{1,0:T(8,128)(2,1)S(1)}, u32[]{:S(2)}, u32[]{:S(2)}) collective-permute-start(bf16[24,3584]{1,0:T(8,128)(2,1)S(1)} %get-tuple-element.18), channel_id=1, source_target_pairs={{0,2},{1,3},{2,0},{3,1},{4,6},{5,7},{6,4},{7,5},{8,10},{9,11},{10,... | collective-permute-start | bytes 516104 | tf_op jit(solution)/shard_map/ppermute | solution.py:24
  34.3 7.4 %collective-permute-start.15 = (bf16[16,8192]{1,0:T(8,128)(2,1)S(1)}, bf16[16,8192]{1,0:T(8,128)(2,1)S(1)}, u32[]{:S(2)}, u32[]{:S(2)}) collective-permute-start(bf16[16,8192]{1,0:T(8,128)(2,1)S(1)} %pad_maximum_fusion.2.rest_8_), channel_id=1, source_target_pairs={{0,12},{1,13},{2,14},{3,15},{4,0},{5,1},{6,2},{7,3},{8,4},{9,5},{1... | collective-permute-start | bytes 786440 | tf_op jit(solution)/shard_map/ppermute | solution.py:24
  40.0 9.4 %collective-permute-start.8 = (bf16[24,4608]{1,0:T(8,128)(2,1)S(1)}, bf16[24,4608]{1,0:T(8,128)(2,1)S(1)}, u32[]{:S(2)}, u32[]{:S(2)}) collective-permute-start(bf16[24,4608]{1,0:T(8,128)(2,1)S(1)} %get-tuple-element.19.rest_4_), channel_id=1, source_target_pairs={{0,4},{1,5},{2,6},{3,7},{4,8},{5,9},{6,10},{7,11},{8,12},{9,13},{1... | collective-permute-start | bytes 663560 | tf_op jit(solution)/shard_map/ppermute | solution.py:24
  41.7 10.5 %collective-permute-start.14 = (bf16[16,8192]{1,0:T(8,128)(2,1)S(1)}, bf16[16,8192]{1,0:T(8,128)(2,1)S(1)}, u32[]{:S(2)}, u32[]{:S(2)}) collective-permute-start(bf16[16,8192]{1,0:T(8,128)(2,1)S(1)} %pad_maximum_fusion.2.rest_8_), channel_id=1, source_target_pairs={{0,4},{1,5},{2,6},{3,7},{4,8},{5,9},{6,10},{7,11},{8,12},{9,13},{1... | collective-permute-start | bytes 786440 | tf_op jit(solution)/shard_map/ppermute | solution.py:24
  49.4 6.0 %collective-permute-start.9 = (bf16[24,4608]{1,0:T(8,128)(2,1)S(1)}, bf16[24,4608]{1,0:T(8,128)(2,1)S(1)}, u32[]{:S(2)}, u32[]{:S(2)}) collective-permute-start(bf16[24,4608]{1,0:T(8,128)(2,1)S(1)} %get-tuple-element.19.rest_4_), channel_id=1, source_target_pairs={{0,12},{1,13},{2,14},{3,15},{4,0},{5,1},{6,2},{7,3},{8,4},{9,5},{1... | collective-permute-start | bytes 663560 | tf_op jit(solution)/shard_map/ppermute | solution.py:24
  52.2 7.4 %collective-permute-start.11 = (bf16[24,4608]{1,0:T(8,128)(2,1)S(1)}, bf16[24,4608]{1,0:T(8,128)(2,1)S(1)}, u32[]{:S(2)}, u32[]{:S(2)}) collective-permute-start(bf16[24,4608]{1,0:T(8,128)(2,1)S(1)} %get-tuple-element.19.rest_4_), channel_id=1, source_target_pairs={{0,2},{1,3},{2,0},{3,1},{4,6},{5,7},{6,4},{7,5},{8,10},{9,11},{10,... | collective-permute-start | bytes 663560 | tf_op jit(solution)/shard_map/ppermute | solution.py:24
  55.5 9.8 %collective-permute-start.10 = (bf16[24,4608]{1,0:T(8,128)(2,1)S(1)}, bf16[24,4608]{1,0:T(8,128)(2,1)S(1)}, u32[]{:S(2)}, u32[]{:S(2)}) collective-permute-start(bf16[24,4608]{1,0:T(8,128)(2,1)S(1)} %get-tuple-element.19.rest_4_), channel_id=1, source_target_pairs={{0,8},{1,9},{2,10},{3,11},{4,12},{5,13},{6,14},{7,15},{8,0},{9,1},... | collective-permute-start | bytes 663560 | tf_op jit(solution)/shard_map/ppermute | solution.py:24
  59.6 10.8 %collective-permute-start.7 = (bf16[48,3584]{1,0:T(8,128)(2,1)S(1)}, bf16[48,3584]{1,0:T(8,128)(2,1)S(1)}, u32[]{:S(2)}, u32[]{:S(2)}) collective-permute-start(bf16[48,3584]{1,0:T(8,128)(2,1)S(1)} %constant_dynamic-update-slice_fusion.rest_0_), channel_id=1, source_target_pairs={{0,8},{1,9},{2,10},{3,11},{4,12},{5,13},{6,14},{7,15},{8,0},{9,1},... | collective-permute-start | bytes 1032200 | tf_op jit(solution)/shard_map/ppermute | solution.py:24
  65.3 10.9 %collective-permute-start.6 = (bf16[48,3584]{1,0:T(8,128)(2,1)S(1)}, bf16[48,3584]{1,0:T(8,128)(2,1)S(1)}, u32[]{:S(2)}, u32[]{:S(2)}) collective-permute-start(bf16[48,3584]{1,0:T(8,128)(2,1)S(1)} %constant_dynamic-update-slice_fusion.rest_0_), channel_id=1, source_target_pairs={{0,12},{1,13},{2,14},{3,15},{4,0},{5,1},{6,2},{7,3},{8,4},{9,5},{1... | collective-permute-start | bytes 1032200 | tf_op jit(solution)/shard_map/ppermute | solution.py:24
  70.4 14.4 %collective-permute-start.12 = (bf16[72,4608]{1,0:T(8,128)(2,1)S(1)}, bf16[72,4608]{1,0:T(8,128)(2,1)S(1)}, u32[]{:S(2)}, u32[]{:S(2)}) collective-permute-start(bf16[72,4608]{1,0:T(8,128)(2,1)S(1)} %constant_dynamic-update-slice_fusion.2.rest_5_), channel_id=1, source_target_pairs={{0,2},{1,3},{2,0},{3,1},{4,6},{5,7},{6,4},{7,5},{8,10},{9,11},{10,... | collective-permute-start | bytes 1990664 | tf_op jit(solution)/shard_map/ppermute | solution.py:24
  76.1 8.5 %collective-permute-start.5 = (bf16[48,3584]{1,0:T(8,128)(2,1)S(1)}, bf16[48,3584]{1,0:T(8,128)(2,1)S(1)}, u32[]{:S(2)}, u32[]{:S(2)}) collective-permute-start(bf16[48,3584]{1,0:T(8,128)(2,1)S(1)} %constant_dynamic-update-slice_fusion.rest_0_), channel_id=1, source_target_pairs={{0,4},{1,5},{2,6},{3,7},{4,8},{5,9},{6,10},{7,11},{8,12},{9,13},{1... | collective-permute-start | bytes 1032200 | tf_op jit(solution)/shard_map/ppermute | solution.py:24
  103.7 8.1 %collective-permute-start.19 = (bf16[24,4096]{1,0:T(8,128)(2,1)S(1)}, bf16[24,4096]{1,0:T(8,128)(2,1)S(1)}, u32[]{:S(2)}, u32[]{:S(2)}) collective-permute-start(bf16[24,4096]{1,0:T(8,128)(2,1)S(1)} %get-tuple-element.24), channel_id=1, source_target_pairs={{0,12},{1,13},{2,14},{3,15},{4,0},{5,1},{6,2},{7,3},{8,4},{9,5},{1... | collective-permute-start | bytes 589832 | tf_op jit(solution)/shard_map/ppermute | solution.py:24
  107.0 10.2 %collective-permute-start.17 = (bf16[24,4096]{1,0:T(8,128)(2,1)S(1)}, bf16[24,4096]{1,0:T(8,128)(2,1)S(1)}, u32[]{:S(2)}, u32[]{:S(2)}) collective-permute-start(bf16[24,4096]{1,0:T(8,128)(2,1)S(1)} %get-tuple-element.22), channel_id=1, source_target_pairs={{0,4},{1,5},{2,6},{3,7},{4,8},{5,9},{6,10},{7,11},{8,12},{9,13},{1... | collective-permute-start | bytes 589832 | tf_op jit(solution)/shard_map/ppermute | solution.py:24
  107.1 13.1 %collective-permute-start.26 = (bf16[16,8192]{1,0:T(8,128)(2,1)S(1)}, bf16[16,8192]{1,0:T(8,128)(2,1)S(1)}, u32[]{:S(2)}, u32[]{:S(2)}) collective-permute-start(bf16[16,8192]{1,0:T(8,128)(2,1)S(1)} %get-tuple-element.28), channel_id=1, source_target_pairs={{0,8},{1,9},{2,10},{3,11},{4,12},{5,13},{6,14},{7,15},{8,0},{9,1},... | collective-permute-start | bytes 786440 | tf_op jit(solution)/shard_map/ppermute | solution.py:24
  108.6 14.1 %collective-permute-start.27 = (bf16[16,8192]{1,0:T(8,128)(2,1)S(1)}, bf16[16,8192]{1,0:T(8,128)(2,1)S(1)}, u32[]{:S(2)}, u32[]{:S(2)}) collective-permute-start(bf16[16,8192]{1,0:T(8,128)(2,1)S(1)} %get-tuple-element.29), channel_id=1, source_target_pairs={{0,4},{1,5},{2,6},{3,7},{4,8},{5,9},{6,10},{7,11},{8,12},{9,13},{1... | collective-permute-start | bytes 786440 | tf_op jit(solution)/shard_map/ppermute | solution.py:24
  111.2 11.5 %collective-permute-start.28 = (bf16[16,8192]{1,0:T(8,128)(2,1)S(1)}, bf16[16,8192]{1,0:T(8,128)(2,1)S(1)}, u32[]{:S(2)}, u32[]{:S(2)}) collective-permute-start(bf16[16,8192]{1,0:T(8,128)(2,1)S(1)} %get-tuple-element.30), channel_id=1, source_target_pairs={{0,12},{1,13},{2,14},{3,15},{4,0},{5,1},{6,2},{7,3},{8,4},{9,5},{1... | collective-permute-start | bytes 786440 | tf_op jit(solution)/shard_map/ppermute | solution.py:24
  111.8 24.7 %collective-permute-start.22 = (bf16[96,4096]{1,0:T(8,128)(2,1)S(1)}, bf16[96,4096]{1,0:T(8,128)(2,1)S(1)}, u32[]{:S(2)}, u32[]{:S(2)}) collective-permute-start(bf16[96,4096]{1,0:T(8,128)(2,1)S(1)} %get-tuple-element.26), channel_id=1, source_target_pairs={{0,2},{1,3},{2,0},{3,1},{4,6},{5,7},{6,4},{7,5},{8,10},{9,11},{10,... | collective-permute-start | bytes 2359304 | tf_op jit(solution)/shard_map/ppermute | solution.py:24
  117.2 12.4 %collective-permute-start.20 = (bf16[48,4096]{1,0:T(8,128)(2,1)S(1)}, bf16[48,4096]{1,0:T(8,128)(2,1)S(1)}, u32[]{:S(2)}, u32[]{:S(2)}) collective-permute-start(bf16[48,4096]{1,0:T(8,128)(2,1)S(1)} %pad_maximum_fusion.1), channel_id=1, source_target_pairs={{0,12},{1,13},{2,14},{3,15},{4,0},{5,1},{6,2},{7,3},{8,4},{9,5},{1... | collective-permute-start | bytes 1179656 | tf_op jit(solution)/shard_map/ppermute | solution.py:24
  120.3 9.3 %collective-permute-start.18 = (bf16[48,4096]{1,0:T(8,128)(2,1)S(1)}, bf16[48,4096]{1,0:T(8,128)(2,1)S(1)}, u32[]{:S(2)}, u32[]{:S(2)}) collective-permute-start(bf16[48,4096]{1,0:T(8,128)(2,1)S(1)} %pad_maximum_fusion), channel_id=1, source_target_pairs={{0,4},{1,5},{2,6},{3,7},{4,8},{5,9},{6,10},{7,11},{8,12},{9,13},{1... | collective-permute-start | bytes 1179656 | tf_op jit(solution)/shard_map/ppermute | solution.py:24
  122.8 30.5 %collective-permute-start.29 = (bf16[8,8192]{1,0:T(8,128)(2,1)S(1)}, bf16[8,8192]{1,0:T(8,128)(2,1)S(1)}, u32[]{:S(2)}, u32[]{:S(2)}) collective-permute-start(bf16[8,8192]{1,0:T(8,128)(2,1)S(1)} %slice.115), channel_id=1, source_target_pairs={{0,2},{1,3},{2,0},{3,1},{4,6},{5,7},{6,4},{7,5},{8,10},{9,11},{10,... | collective-permute-start | bytes 393224 | tf_op jit(solution)/shard_map/ppermute | solution.py:24
  129.8 10.4 %collective-permute-start.21 = (bf16[24,4096]{1,0:T(8,128)(2,1)S(1)}, bf16[24,4096]{1,0:T(8,128)(2,1)S(1)}, u32[]{:S(2)}, u32[]{:S(2)}) collective-permute-start(bf16[24,4096]{1,0:T(8,128)(2,1)S(1)} %slice.114), channel_id=1, source_target_pairs={{0,2},{1,3},{2,0},{3,1},{4,6},{5,7},{6,4},{7,5},{8,10},{9,11},{10,... | collective-permute-start | bytes 589832 | tf_op jit(solution)/shard_map/ppermute | solution.py:24
  136.7 10.6 %collective-permute-start.23 = (bf16[24,4096]{1,0:T(8,128)(2,1)S(1)}, bf16[24,4096]{1,0:T(8,128)(2,1)S(1)}, u32[]{:S(2)}, u32[]{:S(2)}) collective-permute-start(bf16[24,4096]{1,0:T(8,128)(2,1)S(1)} %get-tuple-element.34), channel_id=1, source_target_pairs={{0,4},{1,5},{2,6},{3,7},{4,8},{5,9},{6,10},{7,11},{8,12},{9,13},{1... | collective-permute-start | bytes 589832 | tf_op jit(solution)/shard_map/ppermute | solution.py:24
  136.8 10.5 %collective-permute-start.25 = (bf16[24,4096]{1,0:T(8,128)(2,1)S(1)}, bf16[24,4096]{1,0:T(8,128)(2,1)S(1)}, u32[]{:S(2)}, u32[]{:S(2)}) collective-permute-start(bf16[24,4096]{1,0:T(8,128)(2,1)S(1)} %get-tuple-element.35), channel_id=1, source_target_pairs={{0,8},{1,9},{2,10},{3,11},{4,12},{5,13},{6,14},{7,15},{8,0},{9,1},... | collective-permute-start | bytes 589832 | tf_op jit(solution)/shard_map/ppermute | solution.py:24
  137.8 10.1 %collective-permute-start.24 = (bf16[24,4096]{1,0:T(8,128)(2,1)S(1)}, bf16[24,4096]{1,0:T(8,128)(2,1)S(1)}, u32[]{:S(2)}, u32[]{:S(2)}) collective-permute-start(bf16[24,4096]{1,0:T(8,128)(2,1)S(1)} %get-tuple-element.36), channel_id=1, source_target_pairs={{0,12},{1,13},{2,14},{3,15},{4,0},{5,1},{6,2},{7,3},{8,4},{9,5},{1... | collective-permute-start | bytes 589832 | tf_op jit(solution)/shard_map/ppermute | solution.py:24
  149.6 17.5 %all-to-all-start.1 = ((bf16[8,8,8192]{2,1,0:T(8,128)(2,1)}), bf16[8,8,8192]{2,1,0:T(8,128)(2,1)S(1)}, u32[]{:S(2)}, u32[]{:S(2)}) async-start(bf16[8,8,8192]{2,1,0:T(8,128)(2,1)} %bitcast.9), calls=%async_computation.1 | async-start | bytes 2097152 | tf_op jit(solution)/shard_map/all_to_all | solution.py:286
where the time goes:
time: 170 us; the launch traced here: 169 us
  starting transfers between devices  68.9 us (41%)
  waiting for transfers between devices  67.2 us (40%)
  Pallas kernels  24.2 us (14%)
  other arithmetic  4.11 us (2%)
  local copies, waits for them, and re-layouts  3.46 us (2%)
    ppermute x30, starting transfers between devices, shift(): return lax.ppermute(value, 'mp', shift_pairs(dx, dz, dc))  60.3 us
    ppermute x30, waiting for transfers between devices, shift(): return lax.ppermute(value, 'mp', shift_pairs(dx, dz, dc))  40.6 us
    pallas_call x1, Pallas kernels, run_layer(): pl.pallas_call(functools.partial(layer_kernel, loads, stores, nonzero, ow...  18.9 us
    all_to_all x1, waiting for transfers between devices, run(): lax.all_to_all(returned, 'dp', split_axis=0, concat_axis=0, tiled=True)  13.8 us
    all_to_all x1, waiting for transfers between devices, run(): lax.all_to_all(rolled, 'dp', split_axis=0, concat_axis=0, tiled=True)  12.7 us
    pallas_call x4, Pallas kernels, copy_units(): pl.pallas_call(kernel, in_specs=[pl.BlockSpec(memory_space=pltpu.SMEM)] +...  5.31 us
    all_to_all x1, starting transfers between devices, run(): lax.all_to_all(rolled, 'dp', split_axis=0, concat_axis=0, tiled=True)  4.93 us
    all_to_all x1, starting transfers between devices, run(): lax.all_to_all(returned, 'dp', split_axis=0, concat_axis=0, tiled=True)  3.68 us
  transfers between devices with their start and end apart: 32, of which 17 were waited for; matrix products, arithmetic and copies ran while one was open for 3% of the time, Pallas kernels for 2%

commit v1 on v0

--- a/solution.py
+++ b/solution.py
@@ -47,7 +47,7 @@
             (cross, [(0, 1)]), (three_cross, [(3, 1), (1, 1), (2, 1)])]
 
 
-Z_LAST = [[(2, 0)], [(2, 1)], [(1, 0), (1, 1)], [(3, 0), (3, 1)], [(0, 0), (0, 1)]]
+Z_LAST = [[(2, 0)], [(2, 1)], [(1, 0)], [(1, 1)], [(3, 0)], [(3, 1)], [(0, 0)], [(0, 1)]]
 Z_LAST_DIRECT = [[(dx, 0), (dx, 1)] for dx in (2, 1, 3, 0)]
 Z_FIRST = [[(dx, 1) for dx in range(NX)], [(dx, 0) for dx in range(NX)]]
 
@@ -162,17 +162,15 @@
 
 
 def scatter_z_last(sums):
-    far_0, far_1, next_1, next_3, own = sums
-    rows = far_0.shape[0]
+    far_0, far_1, next_10, next_11, next_30, next_31, own_0, own_1 = sums
     got_0 = shift(far_0, dx=1)
     got_1 = shift(far_1, dx=-1)
-    to_1 = jnp.concatenate([narrow(wide(next_1[:rows]) + wide(got_0)), next_1[rows:]], axis=0)
-    to_3 = jnp.concatenate([next_3[:rows], narrow(wide(next_3[rows:]) + wide(got_1))], axis=0)
-    got_left = shift(to_1, dx=1)
-    got_right = shift(to_3, dx=-1)
-    met = wide(own) + wide(got_left) + wide(got_right)
-    got_z = shift(narrow(met[rows:]), dz=1)
-    return narrow(met[:rows] + wide(got_z))
+    left_1 = shift(next_11, dx=1)
+    right_0 = shift(next_30, dx=-1)
+    left_0 = shift(narrow(wide(next_10) + wide(got_0)), dx=1)
+    right_1 = shift(narrow(wide(next_31) + wide(got_1)), dx=-1)
+    got_z = shift(narrow(wide(own_1) + wide(left_1) + wide(right_1)), dz=1)
+    return narrow(wide(own_0) + wide(left_0) + wide(right_0) + wide(got_z))
 
 
 def scatter_z_last_direct(sums):
@@ -251,7 +249,7 @@
     rows, width = tokens.shape
     block_width = gate_blocks.shape[2]
     width_p = (width // block_width * 7 // 16) * block_width
-    width_sp = (width // block_width * 8 // 16) * block_width
+    width_sp = (width // block_width * 9 // 16) * block_width
     n_dp, firsts, ends, ids, own_first, own_count = plan(row_counts, own_dp, own_mp)
     units = rows // UNIT
     kept_units = units // 2 - 1

time: 170 us -> 176 us (1.035)
  starting transfers between devices: 68.9 us -> 77.5 us
  waiting for transfers between devices: 67.2 us -> 65.4 us
    ppermute x30 -> x32, starting transfers between devices: 60.3 us -> 69 us  [shift(): return lax.ppermute(value, 'mp', shift_pairs(dx, dz, dc))]
    all_to_all x1, waiting for transfers between devices: 13.8 us -> 11.3 us  [run(): lax.all_to_all(returned, 'dp', split_axis=0, concat_axis=0, tiled=True)]
    ppermute x30 -> x32, waiting for transfers between devices: 40.6 us -> 41.4 us  [shift(): return lax.ppermute(value, 'mp', shift_pairs(dx, dz, dc))]
  transfers between devices with their start and end apart: 32 -> 34, of which waited for: 17 -> 18; matrix products, arithmetic and copies ran while one was open for 3% -> 3% of each run, Pallas kernels for 2% -> 2%
where the time goes in v1:
time: 176 us
  starting transfers between devices  77.5 us (44%)
  waiting for transfers between devices  65.4 us (37%)
  Pallas kernels  24.2 us (14%)
  other arithmetic  4.22 us (2%)
  local copies, waits for them, and re-layouts  3.48 us (2%)
    ppermute x32, starting transfers between devices, shift(): return lax.ppermute(value, 'mp', shift_pairs(dx, dz, dc))  69 us
    ppermute x32, waiting for transfers between devices, shift(): return lax.ppermute(value, 'mp', shift_pairs(dx, dz, dc))  41.4 us
    pallas_call x1, Pallas kernels, run_layer(): pl.pallas_call(functools.partial(layer_kernel, loads, stores, nonzero, ow...  18.9 us
    all_to_all x1, waiting for transfers between devices, run(): lax.all_to_all(rolled, 'dp', split_axis=0, concat_axis=0, tiled=True)  12.7 us
    all_to_all x1, waiting for transfers between devices, run(): lax.all_to_all(returned, 'dp', split_axis=0, concat_axis=0, tiled=True)  11.3 us
    pallas_call x4, Pallas kernels, copy_units(): pl.pallas_call(kernel, in_specs=[pl.BlockSpec(memory_space=pltpu.SMEM)] +...  5.31 us
    all_to_all x1, starting transfers between devices, run(): lax.all_to_all(rolled, 'dp', split_axis=0, concat_axis=0, tiled=True)  4.93 us
    all_to_all x1, starting transfers between devices, run(): lax.all_to_all(returned, 'dp', split_axis=0, concat_axis=0, tiled=True)  3.56 us
  transfers between devices with their start and end apart: 34, of which 18 were waited for; matrix products, arithmetic and copies ran while one was open for 3% of the time, Pallas kernels for 2%

profile of v1, /device:TPU:0, one launch (start us, length us, event | category | flops | bytes accessed | tf_op | source)
XLA Modules:
  0.0 175.8 jit_solution(9094576162208031670)
XLA Ops:
  0.0 0.8 pad_add_fusion
  0.8 0.9 slice.46
  1.7 4.1 %collective-permute-start.13 = (bf16[8,8192]{1,0:T(8,128)(2,1)S(1)}, bf16[8,8192]{1,0:T(8,128)(2,1)S(1)}, u32[]{:S(2)}, u32[]{:S(2)}) collective-permute-start(bf16[8,8192]{1,0:T(8,128)(2,1)S(1)} %slice.46), channel_id=1, source_target_pairs={{0,2},{1,3},{2,0},{3,1},{4,6},{5,7},{6,4},{7,5},{8,10},{9,11},{10,... | collective-permute-start | bytes 393224 | tf_op jit(solution)/shard_map/ppermute | solution.py:24
  5.8 0.9 dynamic-slice_reduce_fusion
  6.8 0.7 dynamic_slice.11
  7.5 0.7 fusion.6.table
  8.2 1.2 copy-done
  9.4 1.6 copy_units.4
  11.0 4.9 %all-to-all-start = ((bf16[8,8,8192]{2,1,0:T(8,128)(2,1)}), bf16[8,8,8192]{2,1,0:T(8,128)(2,1)S(1)}, u32[]{:S(2)}, u32[]{:S(2)}) async-start(bf16[8,8,8192]{2,1,0:T(8,128)(2,1)} %bitcast.7), calls=%async_computation | async-start | bytes 2097152 | tf_op jit(solution)/shard_map/all_to_all | solution.py:268
  16.7 3.1 %collective-permute-start.16 = (bf16[16,8192]{1,0:T(8,128)(2,1)S(1)}, bf16[16,8192]{1,0:T(8,128)(2,1)S(1)}, u32[]{:S(2)}, u32[]{:S(2)}) collective-permute-start(bf16[16,8192]{1,0:T(8,128)(2,1)S(1)} %pad_maximum_fusion.rest_8_), channel_id=1, source_target_pairs={{0,8},{1,9},{2,10},{3,11},{4,12},{5,13},{6,14},{7,15},{8,0},{9,1},... | collective-permute-start | bytes 786440 | tf_op jit(solution)/shard_map/ppermute | solution.py:24
  19.8 12.7 %all-to-all-done = bf16[8,8,8192]{2,1,0:T(8,128)(2,1)S(1)} async-done(((bf16[8,8,8192]{2,1,0:T(8,128)(2,1)}), bf16[8,8,8192]{2,1,0:T(8,128)(2,1)S(1)}, u32[]{:S(2)}, u32[]{:S(2)}) %all-to-all-start) | async-done | bytes 1048608 | tf_op jit(solution)/shard_map/all_to_all | solution.py:268
  33.2 1.2 collective-permute-start.4
  34.4 2.8 %collective-permute-start.15 = (bf16[16,8192]{1,0:T(8,128)(2,1)S(1)}, bf16[16,8192]{1,0:T(8,128)(2,1)S(1)}, u32[]{:S(2)}, u32[]{:S(2)}) collective-permute-start(bf16[16,8192]{1,0:T(8,128)(2,1)S(1)} %pad_maximum_fusion.rest_8_), channel_id=1, source_target_pairs={{0,12},{1,13},{2,14},{3,15},{4,0},{5,1},{6,2},{7,3},{8,4},{9,5},{1... | collective-permute-start | bytes 786440 | tf_op jit(solution)/shard_map/ppermute | solution.py:24
  37.3 2.9 %collective-permute-done.4 = bf16[24,3584]{1,0:T(8,128)(2,1)S(1)} collective-permute-done((bf16[24,3584]{1,0:T(8,128)(2,1)S(1)}, bf16[24,3584]{1,0:T(8,128)(2,1)S(1)}, u32[]{:S(2)}, u32[]{:S(2)}) %collective-permute-start.4) | collective-permute-done | bytes 172064 | tf_op jit(solution)/shard_map/ppermute | solution.py:24
  40.2 1.5 collective-permute-start.8
  41.8 1.4 collective-permute-start.14
  43.2 6.3 %collective-permute-done.8 = bf16[24,4608]{1,0:T(8,128)(2,1)S(1)} collective-permute-done((bf16[24,4608]{1,0:T(8,128)(2,1)S(1)}, bf16[24,4608]{1,0:T(8,128)(2,1)S(1)}, u32[]{:S(2)}, u32[]{:S(2)}) %collective-permute-start.8) | collective-permute-done | bytes 221216 | tf_op jit(solution)/shard_map/ppermute | solution.py:24
  49.5 1.7 collective-permute-start.9
  51.2 1.1 collective-permute-done.14.rest_9_
  52.3 1.7 collective-permute-start.11
  54.1 1.5 collective-permute-done.9
  55.6 2.6 %collective-permute-start.10 = (bf16[24,4608]{1,0:T(8,128)(2,1)S(1)}, bf16[24,4608]{1,0:T(8,128)(2,1)S(1)}, u32[]{:S(2)}, u32[]{:S(2)}) collective-permute-start(bf16[24,4608]{1,0:T(8,128)(2,1)S(1)} %get-tuple-element.22.rest_4_), channel_id=1, source_target_pairs={{0,8},{1,9},{2,10},{3,11},{4,12},{5,13},{6,14},{7,15},{8,0},{9,1},... | collective-permute-start | bytes 663560 | tf_op jit(solution)/shard_map/ppermute | solution.py:24
  58.3 1.5 collective-permute-done.11.rest_6_
  59.8 1.8 %collective-permute-start.7 = (bf16[48,3584]{1,0:T(8,128)(2,1)S(1)}, bf16[48,3584]{1,0:T(8,128)(2,1)S(1)}, u32[]{:S(2)}, u32[]{:S(2)}) collective-permute-start(bf16[48,3584]{1,0:T(8,128)(2,1)S(1)} %constant_dynamic-update-slice_fusion.rest_0_), channel_id=1, source_target_pairs={{0,8},{1,9},{2,10},{3,11},{4,12},{5,13},{6,14},{7,15},{8,0},{9,1},... | collective-permute-start | bytes 1032200 | tf_op jit(solution)/shard_map/ppermute | solution.py:24
  61.6 3.8 %collective-permute-done.10 = bf16[24,4608]{1,0:T(8,128)(2,1)S(1)} collective-permute-done((bf16[24,4608]{1,0:T(8,128)(2,1)S(1)}, bf16[24,4608]{1,0:T(8,128)(2,1)S(1)}, u32[]{:S(2)}, u32[]{:S(2)}) %collective-permute-start.10) | collective-permute-done | bytes 221216 | tf_op jit(solution)/shard_map/ppermute | solution.py:24
  65.4 5.1 %collective-permute-start.6 = (bf16[48,3584]{1,0:T(8,128)(2,1)S(1)}, bf16[48,3584]{1,0:T(8,128)(2,1)S(1)}, u32[]{:S(2)}, u32[]{:S(2)}) collective-permute-start(bf16[48,3584]{1,0:T(8,128)(2,1)S(1)} %constant_dynamic-update-slice_fusion.rest_0_), channel_id=1, source_target_pairs={{0,12},{1,13},{2,14},{3,15},{4,0},{5,1},{6,2},{7,3},{8,4},{9,5},{1... | collective-permute-start | bytes 1032200 | tf_op jit(solution)/shard_map/ppermute | solution.py:24
  72.2 4.1 %collective-permute-done.6.rest_2_ = bf16[48,3584]{1,0:T(8,128)(2,1)S(1)} collective-permute-done((bf16[48,3584]{1,0:T(8,128)(2,1)S(1)}, bf16[48,3584]{1,0:T(8,128)(2,1)S(1)}, u32[]{:S(2)}, u32[]{:S(2)}) %collective-permute-start.6) | collective-permute-done | bytes 344096 | tf_op jit(solution)/shard_map/ppermute | solution.py:24
  76.3 0.9 collective-permute-start.5
  77.2 7.5 %collective-permute-done.5.rest_1_ = bf16[48,3584]{1,0:T(8,128)(2,1)S(1)} collective-permute-done((bf16[48,3584]{1,0:T(8,128)(2,1)S(1)}, bf16[48,3584]{1,0:T(8,128)(2,1)S(1)}, u32[]{:S(2)}, u32[]{:S(2)}) %collective-permute-start.5) | collective-permute-done | bytes 344096 | tf_op jit(solution)/shard_map/ppermute | solution.py:24
  84.9 18.9 %sparse_ffn.1 = (bf16[24,4608]{1,0:T(8,128)(2,1)S(1)}, bf16[24,4608]{1,0:T(8,128)(2,1)S(1)}, bf16[24,4608]{1,0:T(8,128)(2,1)S(1)}, bf16[24,4608]{1,0:T(8,128)(2,...) custom-call(s32[8,16]{1,0:T(8,128)S(1)} %get-tuple-element.48.gate_i, ...), custom_call_target="tpu_custom_call" | custom-call | tf_op jit(solution)/shard_map/sparse_ffn/pallas_call | solution.py:130
  103.8 1.0 collective-permute-start.17
  104.8 0.7 and_select_fusion.3
  105.6 2.4 %collective-permute-start.19 = (bf16[24,4608]{1,0:T(8,128)(2,1)S(1)}, bf16[24,4608]{1,0:T(8,128)(2,1)S(1)}, u32[]{:S(2)}, u32[]{:S(2)}) collective-permute-start(bf16[24,4608]{1,0:T(8,128)(2,1)S(1)} %get-tuple-element.26), channel_id=1, source_target_pairs={{0,12},{1,13},{2,14},{3,15},{4,0},{5,1},{6,2},{7,3},{8,4},{9,5},{1... | collective-permute-start | bytes 663560 | tf_op jit(solution)/shard_map/ppermute | solution.py:24
  107.9 3.2 %collective-permute-start.21 = (bf16[24,4608]{1,0:T(8,128)(2,1)S(1)}, bf16[24,4608]{1,0:T(8,128)(2,1)S(1)}, u32[]{:S(2)}, u32[]{:S(2)}) collective-permute-start(bf16[24,4608]{1,0:T(8,128)(2,1)S(1)} %get-tuple-element.30), channel_id=1, source_target_pairs={{0,12},{1,13},{2,14},{3,15},{4,0},{5,1},{6,2},{7,3},{8,4},{9,5},{1... | collective-permute-start | bytes 663560 | tf_op jit(solution)/shard_map/ppermute | solution.py:24
  111.2 4.8 %collective-permute-done.17 = bf16[24,4608]{1,0:T(8,128)(2,1)S(1)} collective-permute-done((bf16[24,4608]{1,0:T(8,128)(2,1)S(1)}, bf16[24,4608]{1,0:T(8,128)(2,1)S(1)}, u32[]{:S(2)}, u32[]{:S(2)}) %collective-permute-start.17) | collective-permute-done | bytes 221216 | tf_op jit(solution)/shard_map/ppermute | solution.py:24
  116.2 4.2 %collective-permute-start.30 = (bf16[16,8192]{1,0:T(8,128)(2,1)S(1)}, bf16[16,8192]{1,0:T(8,128)(2,1)S(1)}, u32[]{:S(2)}, u32[]{:S(2)}) collective-permute-start(bf16[16,8192]{1,0:T(8,128)(2,1)S(1)} %get-tuple-element.36), channel_id=1, source_target_pairs={{0,12},{1,13},{2,14},{3,15},{4,0},{5,1},{6,2},{7,3},{8,4},{9,5},{1... | collective-permute-start | bytes 786440 | tf_op jit(solution)/shard_map/ppermute | solution.py:24
  120.4 2.1 %collective-permute-done.28 = bf16[16,8192]{1,0:T(8,128)(2,1)S(1)} collective-permute-done((bf16[16,8192]{1,0:T(8,128)(2,1)S(1)}, bf16[16,8192]{1,0:T(8,128)(2,1)S(1)}, u32[]{:S(2)}, u32[]{:S(2)}) %collective-permute-start.28) | collective-permute-done | bytes 262176 | tf_op jit(solution)/shard_map/ppermute | solution.py:24
  122.5 7.8 %collective-permute-start.24 = (bf16[96,3584]{1,0:T(8,128)(2,1)S(1)}, bf16[96,3584]{1,0:T(8,128)(2,1)S(1)}, u32[]{:S(2)}, u32[]{:S(2)}) collective-permute-start(bf16[96,3584]{1,0:T(8,128)(2,1)S(1)} %get-tuple-element.32), channel_id=1, source_target_pairs={{0,2},{1,3},{2,0},{3,1},{4,6},{5,7},{6,4},{7,5},{8,10},{9,11},{10,... | collective-permute-start | bytes 2064392 | tf_op jit(solution)/shard_map/ppermute | solution.py:24
  130.4 3.2 %collective-permute-start.22 = (bf16[24,4608]{1,0:T(8,128)(2,1)S(1)}, bf16[24,4608]{1,0:T(8,128)(2,1)S(1)}, u32[]{:S(2)}, u32[]{:S(2)}) collective-permute-start(bf16[24,4608]{1,0:T(8,128)(2,1)S(1)} %add_convert_fusion.2), channel_id=1, source_target_pairs={{0,12},{1,13},{2,14},{3,15},{4,0},{5,1},{6,2},{7,3},{8,4},{9,5},{1... | collective-permute-start | bytes 663560 | tf_op jit(solution)/shard_map/ppermute | solution.py:24
  133.7 6.0 %collective-permute-start.31 = (bf16[8,8192]{1,0:T(8,128)(2,1)S(1)}, bf16[8,8192]{1,0:T(8,128)(2,1)S(1)}, u32[]{:S(2)}, u32[]{:S(2)}) collective-permute-start(bf16[8,8192]{1,0:T(8,128)(2,1)S(1)} %slice.81), channel_id=1, source_target_pairs={{0,2},{1,3},{2,0},{3,1},{4,6},{5,7},{6,4},{7,5},{8,10},{9,11},{10,... | collective-permute-start | bytes 393224 | tf_op jit(solution)/shard_map/ppermute | solution.py:24
  139.9 7.0 %collective-permute-start.23 = (bf16[24,4608]{1,0:T(8,128)(2,1)S(1)}, bf16[24,4608]{1,0:T(8,128)(2,1)S(1)}, u32[]{:S(2)}, u32[]{:S(2)}) collective-permute-start(bf16[24,4608]{1,0:T(8,128)(2,1)S(1)} %add_convert_fusion.1), channel_id=1, source_target_pairs={{0,2},{1,3},{2,0},{3,1},{4,6},{5,7},{6,4},{7,5},{8,10},{9,11},{10,... | collective-permute-start | bytes 663560 | tf_op jit(solution)/shard_map/ppermute | solution.py:24
  147.1 5.1 %collective-permute-start.27 = (bf16[24,3584]{1,0:T(8,128)(2,1)S(1)}, bf16[24,3584]{1,0:T(8,128)(2,1)S(1)}, u32[]{:S(2)}, u32[]{:S(2)}) collective-permute-start(bf16[24,3584]{1,0:T(8,128)(2,1)S(1)} %get-tuple-element.41), channel_id=1, source_target_pairs={{0,8},{1,9},{2,10},{3,11},{4,12},{5,13},{6,14},{7,15},{8,0},{9,1},... | collective-permute-start | bytes 516104 | tf_op jit(solution)/shard_map/ppermute | solution.py:24
  152.3 1.8 %collective-permute-done.25 = bf16[24,3584]{1,0:T(8,128)(2,1)S(1)} collective-permute-done((bf16[24,3584]{1,0:T(8,128)(2,1)S(1)}, bf16[24,3584]{1,0:T(8,128)(2,1)S(1)}, u32[]{:S(2)}, u32[]{:S(2)}) %collective-permute-start.25) | collective-permute-done | bytes 172064 | tf_op jit(solution)/shard_map/ppermute | solution.py:24
  154.1 3.3 %collective-permute-done.27 = bf16[24,3584]{1,0:T(8,128)(2,1)S(1)} collective-permute-done((bf16[24,3584]{1,0:T(8,128)(2,1)S(1)}, bf16[24,3584]{1,0:T(8,128)(2,1)S(1)}, u32[]{:S(2)}, u32[]{:S(2)}) %collective-permute-start.27) | collective-permute-done | bytes 172064 | tf_op jit(solution)/shard_map/ppermute | solution.py:24
  157.7 1.6 copy_units.6
  159.3 3.6 %all-to-all-start.1 = ((bf16[8,8,8192]{2,1,0:T(8,128)(2,1)}), bf16[8,8,8192]{2,1,0:T(8,128)(2,1)S(1)}, u32[]{:S(2)}, u32[]{:S(2)}) async-start(bf16[8,8,8192]{2,1,0:T(8,128)(2,1)} %bitcast.9), calls=%async_computation.1 | async-start | bytes 2097152 | tf_op jit(solution)/shard_map/all_to_all | solution.py:284
  162.9 11.3 %all-to-all-done.1 = bf16[8,8,8192]{2,1,0:T(8,128)(2,1)S(1)} async-done(((bf16[8,8,8192]{2,1,0:T(8,128)(2,1)}), bf16[8,8,8192]{2,1,0:T(8,128)(2,1)S(1)}, u32[]{:S(2)}, u32[]{:S(2)}) %all-to-all-start.1) | async-done | bytes 1048608 | tf_op jit(solution)/shard_map/all_to_all | solution.py:284
  174.2 1.6 copy_units.7
  (64 shorter events, 4.2 us)
Async XLA Ops:
  0.0 77.2 %copy-start.3 = (s32[4,16]{1,0:T(4,128)S(1)}, s32[4,16]{1,0:T(4,128)}, u32[]{:S(2)}) copy-start(s32[4,16]{1,0:T(4,128)} %param.11) | copy-start | bytes 772
  0.0 77.2 %copy-start.2 = (s32[4,16]{1,0:T(4,128)S(1)}, s32[4,16]{1,0:T(4,128)}, u32[]{:S(2)}) copy-start(s32[4,16]{1,0:T(4,128)} %param.13) | copy-start | bytes 772
  0.0 77.2 %copy-start.1 = (s32[4,16]{1,0:T(4,128)S(1)}, s32[4,16]{1,0:T(4,128)}, u32[]{:S(2)}) copy-start(s32[4,16]{1,0:T(4,128)} %param.15) | copy-start | bytes 772
  0.8 32.4 %collective-permute-start = (s32[3,4,16]{2,1,0:T(4,128)S(1)}, s32[3,4,16]{2,1,0:T(4,128)S(1)}, u32[]{:S(2)}, u32[]{:S(2)}) collective-permute-start(s32[3,4,16]{2,1,0:T(4,128)S(1)} %pad_add_fusion), channel_id=1, source_target_pairs={{0,1},{1,0},{2,3},{3,2},{4,5},{5,4},{6,7},{7,6},{8,9},{9,8},{10,11... | collective-permute-start | bytes 2312 | tf_op jit(solution)/shard_map/ppermute | solution.py:24
  1.7 15.0 %collective-permute-start.13 = (bf16[8,8192]{1,0:T(8,128)(2,1)S(1)}, bf16[8,8192]{1,0:T(8,128)(2,1)S(1)}, u32[]{:S(2)}, u32[]{:S(2)}) collective-permute-start(bf16[8,8192]{1,0:T(8,128)(2,1)S(1)} %slice.46), channel_id=1, source_target_pairs={{0,2},{1,3},{2,0},{3,1},{4,6},{5,7},{6,4},{7,5},{8,10},{9,11},{10,... | collective-permute-start | bytes 393224 | tf_op jit(solution)/shard_map/ppermute | solution.py:24
  8.2 1.2 copy-start
  11.0 21.6 %all-to-all-start = ((bf16[8,8,8192]{2,1,0:T(8,128)(2,1)}), bf16[8,8,8192]{2,1,0:T(8,128)(2,1)S(1)}, u32[]{:S(2)}, u32[]{:S(2)}) async-start(bf16[8,8,8192]{2,1,0:T(8,128)(2,1)} %bitcast.7), calls=%async_computation | async-start | bytes 2097152 | tf_op jit(solution)/shard_map/all_to_all | solution.py:268
  15.9 69.0 %collective-permute-start.1 = (bf16[4,16,128,256]{3,2,1,0:T(8,128)(2,1)}, bf16[4,16,128,256]{3,2,1,0:T(8,128)(2,1)}, u32[]{:S(2)}, u32[]{:S(2)}) collective-permute-start(bf16[4,16,128,256]{3,2,1,0:T(8,128)(2,1)} %gate_own.1), channel_id=1, source_target_pairs={{0,1},{1,0},{2,3},{3,2},{4,5},{5,4},{6,7},{7,6},{8,9},{9,8},{10,11... | collective-permute-start | bytes 12582920 | tf_op jit(solution)/shard_map/ppermute | solution.py:24
  15.9 69.0 %collective-permute-start.2 = (bf16[4,16,128,256]{3,2,1,0:T(8,128)(2,1)}, bf16[4,16,128,256]{3,2,1,0:T(8,128)(2,1)}, u32[]{:S(2)}, u32[]{:S(2)}) collective-permute-start(bf16[4,16,128,256]{3,2,1,0:T(8,128)(2,1)} %up_own.1), channel_id=1, source_target_pairs={{0,1},{1,0},{2,3},{3,2},{4,5},{5,4},{6,7},{7,6},{8,9},{9,8},{10,11... | collective-permute-start | bytes 12582920 | tf_op jit(solution)/shard_map/ppermute | solution.py:24
  16.4 68.5 %collective-permute-start.3 = (bf16[4,16,256,128]{3,2,1,0:T(8,128)(2,1)}, bf16[4,16,256,128]{3,2,1,0:T(8,128)(2,1)}, u32[]{:S(2)}, u32[]{:S(2)}) collective-permute-start(bf16[4,16,256,128]{3,2,1,0:T(8,128)(2,1)} %down_own.1), channel_id=1, source_target_pairs={{0,1},{1,0},{2,3},{3,2},{4,5},{5,4},{6,7},{7,6},{8,9},{9,8},{10,11... | collective-permute-start | bytes 12582920 | tf_op jit(solution)/shard_map/ppermute | solution.py:24
  16.7 17.7 %collective-permute-start.16 = (bf16[16,8192]{1,0:T(8,128)(2,1)S(1)}, bf16[16,8192]{1,0:T(8,128)(2,1)S(1)}, u32[]{:S(2)}, u32[]{:S(2)}) collective-permute-start(bf16[16,8192]{1,0:T(8,128)(2,1)S(1)} %pad_maximum_fusion.rest_8_), channel_id=1, source_target_pairs={{0,8},{1,9},{2,10},{3,11},{4,12},{5,13},{6,14},{7,15},{8,0},{9,1},... | collective-permute-start | bytes 786440 | tf_op jit(solution)/shard_map/ppermute | solution.py:24
  33.2 7.0 %collective-permute-start.4 = (bf16[24,3584]{1,0:T(8,128)(2,1)S(1)}, bf16[24,3584]{1,0:T(8,128)(2,1)S(1)}, u32[]{:S(2)}, u32[]{:S(2)}) collective-permute-start(bf16[24,3584]{1,0:T(8,128)(2,1)S(1)} %get-tuple-element.21), channel_id=1, source_target_pairs={{0,2},{1,3},{2,0},{3,1},{4,6},{5,7},{6,4},{7,5},{8,10},{9,11},{10,... | collective-permute-start | bytes 516104 | tf_op jit(solution)/shard_map/ppermute | solution.py:24
  34.4 7.4 %collective-permute-start.15 = (bf16[16,8192]{1,0:T(8,128)(2,1)S(1)}, bf16[16,8192]{1,0:T(8,128)(2,1)S(1)}, u32[]{:S(2)}, u32[]{:S(2)}) collective-permute-start(bf16[16,8192]{1,0:T(8,128)(2,1)S(1)} %pad_maximum_fusion.rest_8_), channel_id=1, source_target_pairs={{0,12},{1,13},{2,14},{3,15},{4,0},{5,1},{6,2},{7,3},{8,4},{9,5},{1... | collective-permute-start | bytes 786440 | tf_op jit(solution)/shard_map/ppermute | solution.py:24
  40.2 9.4 %collective-permute-start.8 = (bf16[24,4608]{1,0:T(8,128)(2,1)S(1)}, bf16[24,4608]{1,0:T(8,128)(2,1)S(1)}, u32[]{:S(2)}, u32[]{:S(2)}) collective-permute-start(bf16[24,4608]{1,0:T(8,128)(2,1)S(1)} %get-tuple-element.22.rest_4_), channel_id=1, source_target_pairs={{0,4},{1,5},{2,6},{3,7},{4,8},{5,9},{6,10},{7,11},{8,12},{9,13},{1... | collective-permute-start | bytes 663560 | tf_op jit(solution)/shard_map/ppermute | solution.py:24
  41.8 10.5 %collective-permute-start.14 = (bf16[16,8192]{1,0:T(8,128)(2,1)S(1)}, bf16[16,8192]{1,0:T(8,128)(2,1)S(1)}, u32[]{:S(2)}, u32[]{:S(2)}) collective-permute-start(bf16[16,8192]{1,0:T(8,128)(2,1)S(1)} %pad_maximum_fusion.rest_8_), channel_id=1, source_target_pairs={{0,4},{1,5},{2,6},{3,7},{4,8},{5,9},{6,10},{7,11},{8,12},{9,13},{1... | collective-permute-start | bytes 786440 | tf_op jit(solution)/shard_map/ppermute | solution.py:24
  49.5 6.0 %collective-permute-start.9 = (bf16[24,4608]{1,0:T(8,128)(2,1)S(1)}, bf16[24,4608]{1,0:T(8,128)(2,1)S(1)}, u32[]{:S(2)}, u32[]{:S(2)}) collective-permute-start(bf16[24,4608]{1,0:T(8,128)(2,1)S(1)} %get-tuple-element.22.rest_4_), channel_id=1, source_target_pairs={{0,12},{1,13},{2,14},{3,15},{4,0},{5,1},{6,2},{7,3},{8,4},{9,5},{1... | collective-permute-start | bytes 663560 | tf_op jit(solution)/shard_map/ppermute | solution.py:24
  52.3 7.4 %collective-permute-start.11 = (bf16[24,4608]{1,0:T(8,128)(2,1)S(1)}, bf16[24,4608]{1,0:T(8,128)(2,1)S(1)}, u32[]{:S(2)}, u32[]{:S(2)}) collective-permute-start(bf16[24,4608]{1,0:T(8,128)(2,1)S(1)} %get-tuple-element.22.rest_4_), channel_id=1, source_target_pairs={{0,2},{1,3},{2,0},{3,1},{4,6},{5,7},{6,4},{7,5},{8,10},{9,11},{10,... | collective-permute-start | bytes 663560 | tf_op jit(solution)/shard_map/ppermute | solution.py:24
  55.6 9.8 %collective-permute-start.10 = (bf16[24,4608]{1,0:T(8,128)(2,1)S(1)}, bf16[24,4608]{1,0:T(8,128)(2,1)S(1)}, u32[]{:S(2)}, u32[]{:S(2)}) collective-permute-start(bf16[24,4608]{1,0:T(8,128)(2,1)S(1)} %get-tuple-element.22.rest_4_), channel_id=1, source_target_pairs={{0,8},{1,9},{2,10},{3,11},{4,12},{5,13},{6,14},{7,15},{8,0},{9,1},... | collective-permute-start | bytes 663560 | tf_op jit(solution)/shard_map/ppermute | solution.py:24
  59.8 10.8 %collective-permute-start.7 = (bf16[48,3584]{1,0:T(8,128)(2,1)S(1)}, bf16[48,3584]{1,0:T(8,128)(2,1)S(1)}, u32[]{:S(2)}, u32[]{:S(2)}) collective-permute-start(bf16[48,3584]{1,0:T(8,128)(2,1)S(1)} %constant_dynamic-update-slice_fusion.rest_0_), channel_id=1, source_target_pairs={{0,8},{1,9},{2,10},{3,11},{4,12},{5,13},{6,14},{7,15},{8,0},{9,1},... | collective-permute-start | bytes 1032200 | tf_op jit(solution)/shard_map/ppermute | solution.py:24
  65.4 10.9 %collective-permute-start.6 = (bf16[48,3584]{1,0:T(8,128)(2,1)S(1)}, bf16[48,3584]{1,0:T(8,128)(2,1)S(1)}, u32[]{:S(2)}, u32[]{:S(2)}) collective-permute-start(bf16[48,3584]{1,0:T(8,128)(2,1)S(1)} %constant_dynamic-update-slice_fusion.rest_0_), channel_id=1, source_target_pairs={{0,12},{1,13},{2,14},{3,15},{4,0},{5,1},{6,2},{7,3},{8,4},{9,5},{1... | collective-permute-start | bytes 1032200 | tf_op jit(solution)/shard_map/ppermute | solution.py:24
  70.6 14.4 %collective-permute-start.12 = (bf16[72,4608]{1,0:T(8,128)(2,1)S(1)}, bf16[72,4608]{1,0:T(8,128)(2,1)S(1)}, u32[]{:S(2)}, u32[]{:S(2)}) collective-permute-start(bf16[72,4608]{1,0:T(8,128)(2,1)S(1)} %constant_dynamic-update-slice_fusion.2.rest_5_), channel_id=1, source_target_pairs={{0,2},{1,3},{2,0},{3,1},{4,6},{5,7},{6,4},{7,5},{8,10},{9,11},{10,... | collective-permute-start | bytes 1990664 | tf_op jit(solution)/shard_map/ppermute | solution.py:24
  76.3 8.5 %collective-permute-start.5 = (bf16[48,3584]{1,0:T(8,128)(2,1)S(1)}, bf16[48,3584]{1,0:T(8,128)(2,1)S(1)}, u32[]{:S(2)}, u32[]{:S(2)}) collective-permute-start(bf16[48,3584]{1,0:T(8,128)(2,1)S(1)} %constant_dynamic-update-slice_fusion.rest_0_), channel_id=1, source_target_pairs={{0,4},{1,5},{2,6},{3,7},{4,8},{5,9},{6,10},{7,11},{8,12},{9,13},{1... | collective-permute-start | bytes 1032200 | tf_op jit(solution)/shard_map/ppermute | solution.py:24
  103.8 12.1 %collective-permute-start.17 = (bf16[24,4608]{1,0:T(8,128)(2,1)S(1)}, bf16[24,4608]{1,0:T(8,128)(2,1)S(1)}, u32[]{:S(2)}, u32[]{:S(2)}) collective-permute-start(bf16[24,4608]{1,0:T(8,128)(2,1)S(1)} %get-tuple-element.25), channel_id=1, source_target_pairs={{0,4},{1,5},{2,6},{3,7},{4,8},{5,9},{6,10},{7,11},{8,12},{9,13},{1... | collective-permute-start | bytes 663560 | tf_op jit(solution)/shard_map/ppermute | solution.py:24
  105.6 41.5 %collective-permute-start.19 = (bf16[24,4608]{1,0:T(8,128)(2,1)S(1)}, bf16[24,4608]{1,0:T(8,128)(2,1)S(1)}, u32[]{:S(2)}, u32[]{:S(2)}) collective-permute-start(bf16[24,4608]{1,0:T(8,128)(2,1)S(1)} %get-tuple-element.26), channel_id=1, source_target_pairs={{0,12},{1,13},{2,14},{3,15},{4,0},{5,1},{6,2},{7,3},{8,4},{9,5},{1... | collective-permute-start | bytes 663560 | tf_op jit(solution)/shard_map/ppermute | solution.py:24
  107.9 25.8 %collective-permute-start.20 = (bf16[24,4608]{1,0:T(8,128)(2,1)S(1)}, bf16[24,4608]{1,0:T(8,128)(2,1)S(1)}, u32[]{:S(2)}, u32[]{:S(2)}) collective-permute-start(bf16[24,4608]{1,0:T(8,128)(2,1)S(1)} %get-tuple-element.28), channel_id=1, source_target_pairs={{0,4},{1,5},{2,6},{3,7},{4,8},{5,9},{6,10},{7,11},{8,12},{9,13},{1... | collective-permute-start | bytes 663560 | tf_op jit(solution)/shard_map/ppermute | solution.py:24
  107.9 8.2 %collective-permute-start.21 = (bf16[24,4608]{1,0:T(8,128)(2,1)S(1)}, bf16[24,4608]{1,0:T(8,128)(2,1)S(1)}, u32[]{:S(2)}, u32[]{:S(2)}) collective-permute-start(bf16[24,4608]{1,0:T(8,128)(2,1)S(1)} %get-tuple-element.30), channel_id=1, source_target_pairs={{0,12},{1,13},{2,14},{3,15},{4,0},{5,1},{6,2},{7,3},{8,4},{9,5},{1... | collective-permute-start | bytes 663560 | tf_op jit(solution)/shard_map/ppermute | solution.py:24
  111.2 11.3 %collective-permute-start.28 = (bf16[16,8192]{1,0:T(8,128)(2,1)S(1)}, bf16[16,8192]{1,0:T(8,128)(2,1)S(1)}, u32[]{:S(2)}, u32[]{:S(2)}) collective-permute-start(bf16[16,8192]{1,0:T(8,128)(2,1)S(1)} %get-tuple-element.34), channel_id=1, source_target_pairs={{0,8},{1,9},{2,10},{3,11},{4,12},{5,13},{6,14},{7,15},{8,0},{9,1},... | collective-permute-start | bytes 786440 | tf_op jit(solution)/shard_map/ppermute | solution.py:24
  116.0 14.4 %collective-permute-start.29 = (bf16[16,8192]{1,0:T(8,128)(2,1)S(1)}, bf16[16,8192]{1,0:T(8,128)(2,1)S(1)}, u32[]{:S(2)}, u32[]{:S(2)}) collective-permute-start(bf16[16,8192]{1,0:T(8,128)(2,1)S(1)} %get-tuple-element.35), channel_id=1, source_target_pairs={{0,4},{1,5},{2,6},{3,7},{4,8},{5,9},{6,10},{7,11},{8,12},{9,13},{1... | collective-permute-start | bytes 786440 | tf_op jit(solution)/shard_map/ppermute | solution.py:24
  116.2 14.2 %collective-permute-start.30 = (bf16[16,8192]{1,0:T(8,128)(2,1)S(1)}, bf16[16,8192]{1,0:T(8,128)(2,1)S(1)}, u32[]{:S(2)}, u32[]{:S(2)}) collective-permute-start(bf16[16,8192]{1,0:T(8,128)(2,1)S(1)} %get-tuple-element.36), channel_id=1, source_target_pairs={{0,12},{1,13},{2,14},{3,15},{4,0},{5,1},{6,2},{7,3},{8,4},{9,5},{1... | collective-permute-start | bytes 786440 | tf_op jit(solution)/shard_map/ppermute | solution.py:24
  122.5 24.4 %collective-permute-start.24 = (bf16[96,3584]{1,0:T(8,128)(2,1)S(1)}, bf16[96,3584]{1,0:T(8,128)(2,1)S(1)}, u32[]{:S(2)}, u32[]{:S(2)}) collective-permute-start(bf16[96,3584]{1,0:T(8,128)(2,1)S(1)} %get-tuple-element.32), channel_id=1, source_target_pairs={{0,2},{1,3},{2,0},{3,1},{4,6},{5,7},{6,4},{7,5},{8,10},{9,11},{10,... | collective-permute-start | bytes 2064392 | tf_op jit(solution)/shard_map/ppermute | solution.py:24
  130.3 21.8 %collective-permute-start.18 = (bf16[24,4608]{1,0:T(8,128)(2,1)S(1)}, bf16[24,4608]{1,0:T(8,128)(2,1)S(1)}, u32[]{:S(2)}, u32[]{:S(2)}) collective-permute-start(bf16[24,4608]{1,0:T(8,128)(2,1)S(1)} %add_convert_fusion.3), channel_id=1, source_target_pairs={{0,4},{1,5},{2,6},{3,7},{4,8},{5,9},{6,10},{7,11},{8,12},{9,13},{1... | collective-permute-start | bytes 663560 | tf_op jit(solution)/shard_map/ppermute | solution.py:24
  130.4 9.4 %collective-permute-start.22 = (bf16[24,4608]{1,0:T(8,128)(2,1)S(1)}, bf16[24,4608]{1,0:T(8,128)(2,1)S(1)}, u32[]{:S(2)}, u32[]{:S(2)}) collective-permute-start(bf16[24,4608]{1,0:T(8,128)(2,1)S(1)} %add_convert_fusion.2), channel_id=1, source_target_pairs={{0,12},{1,13},{2,14},{3,15},{4,0},{5,1},{6,2},{7,3},{8,4},{9,5},{1... | collective-permute-start | bytes 663560 | tf_op jit(solution)/shard_map/ppermute | solution.py:24
  133.7 29.1 %collective-permute-start.31 = (bf16[8,8192]{1,0:T(8,128)(2,1)S(1)}, bf16[8,8192]{1,0:T(8,128)(2,1)S(1)}, u32[]{:S(2)}, u32[]{:S(2)}) collective-permute-start(bf16[8,8192]{1,0:T(8,128)(2,1)S(1)} %slice.81), channel_id=1, source_target_pairs={{0,2},{1,3},{2,0},{3,1},{4,6},{5,7},{6,4},{7,5},{8,10},{9,11},{10,... | collective-permute-start | bytes 393224 | tf_op jit(solution)/shard_map/ppermute | solution.py:24
  139.9 12.3 %collective-permute-start.23 = (bf16[24,4608]{1,0:T(8,128)(2,1)S(1)}, bf16[24,4608]{1,0:T(8,128)(2,1)S(1)}, u32[]{:S(2)}, u32[]{:S(2)}) collective-permute-start(bf16[24,4608]{1,0:T(8,128)(2,1)S(1)} %add_convert_fusion.1), channel_id=1, source_target_pairs={{0,2},{1,3},{2,0},{3,1},{4,6},{5,7},{6,4},{7,5},{8,10},{9,11},{10,... | collective-permute-start | bytes 663560 | tf_op jit(solution)/shard_map/ppermute | solution.py:24
  147.0 7.1 %collective-permute-start.25 = (bf16[24,3584]{1,0:T(8,128)(2,1)S(1)}, bf16[24,3584]{1,0:T(8,128)(2,1)S(1)}, u32[]{:S(2)}, u32[]{:S(2)}) collective-permute-start(bf16[24,3584]{1,0:T(8,128)(2,1)S(1)} %get-tuple-element.40), channel_id=1, source_target_pairs={{0,4},{1,5},{2,6},{3,7},{4,8},{5,9},{6,10},{7,11},{8,12},{9,13},{1... | collective-permute-start | bytes 516104 | tf_op jit(solution)/shard_map/ppermute | solution.py:24
  147.1 10.3 %collective-permute-start.27 = (bf16[24,3584]{1,0:T(8,128)(2,1)S(1)}, bf16[24,3584]{1,0:T(8,128)(2,1)S(1)}, u32[]{:S(2)}, u32[]{:S(2)}) collective-permute-start(bf16[24,3584]{1,0:T(8,128)(2,1)S(1)} %get-tuple-element.41), channel_id=1, source_target_pairs={{0,8},{1,9},{2,10},{3,11},{4,12},{5,13},{6,14},{7,15},{8,0},{9,1},... | collective-permute-start | bytes 516104 | tf_op jit(solution)/shard_map/ppermute | solution.py:24
  152.2 5.4 %collective-permute-start.26 = (bf16[24,3584]{1,0:T(8,128)(2,1)S(1)}, bf16[24,3584]{1,0:T(8,128)(2,1)S(1)}, u32[]{:S(2)}, u32[]{:S(2)}) collective-permute-start(bf16[24,3584]{1,0:T(8,128)(2,1)S(1)} %get-tuple-element.42), channel_id=1, source_target_pairs={{0,12},{1,13},{2,14},{3,15},{4,0},{5,1},{6,2},{7,3},{8,4},{9,5},{1... | collective-permute-start | bytes 516104 | tf_op jit(solution)/shard_map/ppermute | solution.py:24
  159.3 14.9 %all-to-all-start.1 = ((bf16[8,8,8192]{2,1,0:T(8,128)(2,1)}), bf16[8,8,8192]{2,1,0:T(8,128)(2,1)S(1)}, u32[]{:S(2)}, u32[]{:S(2)}) async-start(bf16[8,8,8192]{2,1,0:T(8,128)(2,1)} %bitcast.9), calls=%async_computation.1 | async-start | bytes 2097152 | tf_op jit(solution)/shard_map/all_to_all | solution.py:284

commit v2 on v1

--- a/solution.py
+++ b/solution.py
@@ -48,7 +48,6 @@
 
 
 Z_LAST = [[(2, 0)], [(2, 1)], [(1, 0)], [(1, 1)], [(3, 0)], [(3, 1)], [(0, 0)], [(0, 1)]]
-Z_LAST_DIRECT = [[(dx, 0), (dx, 1)] for dx in (2, 1, 3, 0)]
 Z_FIRST = [[(dx, 1) for dx in range(NX)], [(dx, 0) for dx in range(NX)]]
 
 
@@ -174,12 +173,16 @@
 
 
 def scatter_z_last_direct(sums):
-    far, next_1, next_3, own = sums
-    rows = far.shape[0] // 2
-    got = [shift(far, dx=2), shift(next_1, dx=1), shift(next_3, dx=-1)]
-    met = wide(own) + wide(got[0]) + wide(got[1]) + wide(got[2])
-    got_z = shift(narrow(met[rows:]), dz=1)
-    return narrow(met[:rows] + wide(got_z))
+    far_0, far_1, next_10, next_11, next_30, next_31, own_0, own_1 = sums
+
+    def meet(own, next_1, next_3, far):
+        got = [shift(next_1, dx=1), shift(next_3, dx=-1),
+               shift(far, dx=2)]
+        return wide(own) + wide(got[0]) + wide(got[1]) + wide(got[2])
+
+    crossing = narrow(meet(own_1, next_11, next_31, far_1))
+    got_z = shift(crossing, dz=1)
+    return narrow(meet(own_0, next_10, next_30, far_0) + wide(got_z))
 
 
 def scatter_z_first(sums):
@@ -274,7 +277,7 @@
     sent_parts = [
         (Z_LAST, kept, 0, 0, width_sp),
         (Z_FIRST, kept, 0, width_sp, width - width_sp),
-        (Z_LAST_DIRECT, UNIT, 8 * kept, 0, width),
+        (Z_LAST, UNIT, 8 * kept, 0, width),
     ]
     sums_p, sums_q, sums_still = run_layer(
         gathered_parts, sent_parts, width, index_own, index_other, weights_own, weights_other)

time: 176 us -> 182 us (1.034)
  waiting for transfers between devices: 65.4 us -> 81.3 us
  starting transfers between devices: 77.5 us -> 67.2 us
    ppermute x32 -> x35, waiting for transfers between devices: 41.4 us -> 59.9 us  [shift(): return lax.ppermute(value, 'mp', shift_pairs(dx, dz, dc))]
    ppermute x32 -> x35, starting transfers between devices: 69 us -> 56.8 us  [shift(): return lax.ppermute(value, 'mp', shift_pairs(dx, dz, dc))]
    all_to_all x1, waiting for transfers between devices: 11.3 us -> 8.62 us  [run(): lax.all_to_all(returned, 'dp', split_axis=0, concat_axis=0, tiled=True)]
    all_to_all x1, starting transfers between devices: 3.56 us -> 5.48 us  [run(): lax.all_to_all(returned, 'dp', split_axis=0, concat_axis=0, tiled=True)]
  transfers between devices with their start and end apart: 34 -> 37, of which waited for: 18 -> 19; matrix products, arithmetic and copies ran while one was open for 3% -> 3% of each run, Pallas kernels for 2% -> 2%
where the time goes in v2:
time: 182 us; the launch traced here: 181 us
  waiting for transfers between devices  81.3 us (45%)
  starting transfers between devices  67.2 us (37%)
  Pallas kernels  24.2 us (13%)
  other arithmetic  4.2 us (2%)
  local copies, waits for them, and re-layouts  3.47 us (2%)
    ppermute x35, waiting for transfers between devices, shift(): return lax.ppermute(value, 'mp', shift_pairs(dx, dz, dc))  59.9 us
    ppermute x35, starting transfers between devices, shift(): return lax.ppermute(value, 'mp', shift_pairs(dx, dz, dc))  56.8 us
    pallas_call x1, Pallas kernels, run_layer(): pl.pallas_call(functools.partial(layer_kernel, loads, stores, nonzero, ow...  18.9 us
    all_to_all x1, waiting for transfers between devices, run(): lax.all_to_all(rolled, 'dp', split_axis=0, concat_axis=0, tiled=True)  12.7 us
    all_to_all x1, waiting for transfers between devices, run(): lax.all_to_all(returned, 'dp', split_axis=0, concat_axis=0, tiled=True)  8.62 us
    all_to_all x1, starting transfers between devices, run(): lax.all_to_all(returned, 'dp', split_axis=0, concat_axis=0, tiled=True)  5.48 us
    pallas_call x4, Pallas kernels, copy_units(): pl.pallas_call(kernel, in_specs=[pl.BlockSpec(memory_space=pltpu.SMEM)] +...  5.31 us
    all_to_all x1, starting transfers between devices, run(): lax.all_to_all(rolled, 'dp', split_axis=0, concat_axis=0, tiled=True)  4.93 us
  transfers between devices with their start and end apart: 37, of which 19 were waited for; matrix products, arithmetic and copies ran while one was open for 3% of the time, Pallas kernels for 2%

profile of v2, /device:TPU:0, one launch (start us, length us, event | category | flops | bytes accessed | tf_op | source)
XLA Modules:
  0.0 181.2 jit_solution(9471989787458046273)
XLA Ops:
  0.0 0.8 pad_add_fusion
  0.8 0.9 slice.39
  1.7 4.1 %collective-permute-start.13 = (bf16[8,8192]{1,0:T(8,128)(2,1)S(1)}, bf16[8,8192]{1,0:T(8,128)(2,1)S(1)}, u32[]{:S(2)}, u32[]{:S(2)}) collective-permute-start(bf16[8,8192]{1,0:T(8,128)(2,1)S(1)} %slice.39), channel_id=1, source_target_pairs={{0,2},{1,3},{2,0},{3,1},{4,6},{5,7},{6,4},{7,5},{8,10},{9,11},{10,... | collective-permute-start | bytes 393224 | tf_op jit(solution)/shard_map/ppermute | solution.py:24
  5.8 0.9 dynamic-slice_reduce_fusion
  8.2 1.2 copy-done
  9.4 1.6 copy_units.4
  11.0 4.9 %all-to-all-start = ((bf16[8,8,8192]{2,1,0:T(8,128)(2,1)}), bf16[8,8,8192]{2,1,0:T(8,128)(2,1)S(1)}, u32[]{:S(2)}, u32[]{:S(2)}) async-start(bf16[8,8,8192]{2,1,0:T(8,128)(2,1)} %bitcast.7), calls=%async_computation | async-start | bytes 2097152 | tf_op jit(solution)/shard_map/all_to_all | solution.py:271
  16.7 3.1 %collective-permute-start.16 = (bf16[16,8192]{1,0:T(8,128)(2,1)S(1)}, bf16[16,8192]{1,0:T(8,128)(2,1)S(1)}, u32[]{:S(2)}, u32[]{:S(2)}) collective-permute-start(bf16[16,8192]{1,0:T(8,128)(2,1)S(1)} %pad_maximum_fusion.rest_8_), channel_id=1, source_target_pairs={{0,8},{1,9},{2,10},{3,11},{4,12},{5,13},{6,14},{7,15},{8,0},{9,1},... | collective-permute-start | bytes 786440 | tf_op jit(solution)/shard_map/ppermute | solution.py:24
  19.8 12.7 %all-to-all-done = bf16[8,8,8192]{2,1,0:T(8,128)(2,1)S(1)} async-done(((bf16[8,8,8192]{2,1,0:T(8,128)(2,1)}), bf16[8,8,8192]{2,1,0:T(8,128)(2,1)S(1)}, u32[]{:S(2)}, u32[]{:S(2)}) %all-to-all-start) | async-done | bytes 1048608 | tf_op jit(solution)/shard_map/all_to_all | solution.py:271
  33.2 1.2 collective-permute-start.4
  34.4 2.8 %collective-permute-start.15 = (bf16[16,8192]{1,0:T(8,128)(2,1)S(1)}, bf16[16,8192]{1,0:T(8,128)(2,1)S(1)}, u32[]{:S(2)}, u32[]{:S(2)}) collective-permute-start(bf16[16,8192]{1,0:T(8,128)(2,1)S(1)} %pad_maximum_fusion.rest_8_), channel_id=1, source_target_pairs={{0,12},{1,13},{2,14},{3,15},{4,0},{5,1},{6,2},{7,3},{8,4},{9,5},{1... | collective-permute-start | bytes 786440 | tf_op jit(solution)/shard_map/ppermute | solution.py:24
  37.3 2.9 %collective-permute-done.4 = bf16[24,3584]{1,0:T(8,128)(2,1)S(1)} collective-permute-done((bf16[24,3584]{1,0:T(8,128)(2,1)S(1)}, bf16[24,3584]{1,0:T(8,128)(2,1)S(1)}, u32[]{:S(2)}, u32[]{:S(2)}) %collective-permute-start.4) | collective-permute-done | bytes 172064 | tf_op jit(solution)/shard_map/ppermute | solution.py:24
  40.2 1.5 collective-permute-start.8
  41.8 1.4 collective-permute-start.14
  43.2 6.3 %collective-permute-done.8 = bf16[24,4608]{1,0:T(8,128)(2,1)S(1)} collective-permute-done((bf16[24,4608]{1,0:T(8,128)(2,1)S(1)}, bf16[24,4608]{1,0:T(8,128)(2,1)S(1)}, u32[]{:S(2)}, u32[]{:S(2)}) %collective-permute-start.8) | collective-permute-done | bytes 221216 | tf_op jit(solution)/shard_map/ppermute | solution.py:24
  49.5 1.7 collective-permute-start.9
  51.2 1.1 collective-permute-done.14.rest_9_
  52.3 1.7 collective-permute-start.11
  54.1 1.5 collective-permute-done.9
  55.6 2.6 %collective-permute-start.10 = (bf16[24,4608]{1,0:T(8,128)(2,1)S(1)}, bf16[24,4608]{1,0:T(8,128)(2,1)S(1)}, u32[]{:S(2)}, u32[]{:S(2)}) collective-permute-start(bf16[24,4608]{1,0:T(8,128)(2,1)S(1)} %get-tuple-element.26.rest_4_), channel_id=1, source_target_pairs={{0,8},{1,9},{2,10},{3,11},{4,12},{5,13},{6,14},{7,15},{8,0},{9,1},... | collective-permute-start | bytes 663560 | tf_op jit(solution)/shard_map/ppermute | solution.py:24
  58.2 1.5 collective-permute-done.11.rest_6_
  59.8 1.8 collective-permute-start.7
  61.5 3.8 %collective-permute-done.10 = bf16[24,4608]{1,0:T(8,128)(2,1)S(1)} collective-permute-done((bf16[24,4608]{1,0:T(8,128)(2,1)S(1)}, bf16[24,4608]{1,0:T(8,128)(2,1)S(1)}, u32[]{:S(2)}, u32[]{:S(2)}) %collective-permute-start.10) | collective-permute-done | bytes 221216 | tf_op jit(solution)/shard_map/ppermute | solution.py:24
  65.4 5.1 %collective-permute-start.6 = (bf16[48,3584]{1,0:T(8,128)(2,1)S(1)}, bf16[48,3584]{1,0:T(8,128)(2,1)S(1)}, u32[]{:S(2)}, u32[]{:S(2)}) collective-permute-start(bf16[48,3584]{1,0:T(8,128)(2,1)S(1)} %constant_dynamic-update-slice_fusion.rest_0_), channel_id=1, source_target_pairs={{0,12},{1,13},{2,14},{3,15},{4,0},{5,1},{6,2},{7,3},{8,4},{9,5},{1... | collective-permute-start | bytes 1032200 | tf_op jit(solution)/shard_map/ppermute | solution.py:24
  70.9 5.3 %collective-permute-done.6.rest_2_ = bf16[48,3584]{1,0:T(8,128)(2,1)S(1)} collective-permute-done((bf16[48,3584]{1,0:T(8,128)(2,1)S(1)}, bf16[48,3584]{1,0:T(8,128)(2,1)S(1)}, u32[]{:S(2)}, u32[]{:S(2)}) %collective-permute-start.6) | collective-permute-done | bytes 344096 | tf_op jit(solution)/shard_map/ppermute | solution.py:24
  76.3 0.9 collective-permute-start.5
  77.2 7.5 %collective-permute-done.5.rest_1_ = bf16[48,3584]{1,0:T(8,128)(2,1)S(1)} collective-permute-done((bf16[48,3584]{1,0:T(8,128)(2,1)S(1)}, bf16[48,3584]{1,0:T(8,128)(2,1)S(1)}, u32[]{:S(2)}, u32[]{:S(2)}) %collective-permute-start.5) | collective-permute-done | bytes 344096 | tf_op jit(solution)/shard_map/ppermute | solution.py:24
  84.9 18.9 %sparse_ffn.1 = (bf16[24,4608]{1,0:T(8,128)(2,1)S(1)}, bf16[24,4608]{1,0:T(8,128)(2,1)S(1)}, bf16[24,4608]{1,0:T(8,128)(2,1)S(1)}, bf16[24,4608]{1,0:T(8,128)(2,...) custom-call(s32[8,16]{1,0:T(8,128)S(1)} %get-tuple-element.56.gate_i, ...), custom_call_target="tpu_custom_call" | custom-call | tf_op jit(solution)/shard_map/sparse_ffn/pallas_call | solution.py:129
  103.8 1.0 collective-permute-start.31
  104.8 2.3 %collective-permute-start.32 = (bf16[8,8192]{1,0:T(8,128)(2,1)S(1)}, bf16[8,8192]{1,0:T(8,128)(2,1)S(1)}, u32[]{:S(2)}, u32[]{:S(2)}) collective-permute-start(bf16[8,8192]{1,0:T(8,128)(2,1)S(1)} %get-tuple-element.43), channel_id=1, source_target_pairs={{0,12},{1,13},{2,14},{3,15},{4,0},{5,1},{6,2},{7,3},{8,4},{9,5},{1... | collective-permute-start | bytes 393224 | tf_op jit(solution)/shard_map/ppermute | solution.py:24
  109.9 1.4 collective-permute-start.28
  111.3 1.8 %collective-permute-start.29 = (bf16[8,8192]{1,0:T(8,128)(2,1)S(1)}, bf16[8,8192]{1,0:T(8,128)(2,1)S(1)}, u32[]{:S(2)}, u32[]{:S(2)}) collective-permute-start(bf16[8,8192]{1,0:T(8,128)(2,1)S(1)} %get-tuple-element.39), channel_id=1, source_target_pairs={{0,12},{1,13},{2,14},{3,15},{4,0},{5,1},{6,2},{7,3},{8,4},{9,5},{1... | collective-permute-start | bytes 393224 | tf_op jit(solution)/shard_map/ppermute | solution.py:24
  113.4 3.0 %collective-permute-start.19 = (bf16[24,4608]{1,0:T(8,128)(2,1)S(1)}, bf16[24,4608]{1,0:T(8,128)(2,1)S(1)}, u32[]{:S(2)}, u32[]{:S(2)}) collective-permute-start(bf16[24,4608]{1,0:T(8,128)(2,1)S(1)} %get-tuple-element.30), channel_id=1, source_target_pairs={{0,12},{1,13},{2,14},{3,15},{4,0},{5,1},{6,2},{7,3},{8,4},{9,5},{1... | collective-permute-start | bytes 663560 | tf_op jit(solution)/shard_map/ppermute | solution.py:24
  116.7 6.4 %collective-permute-done.21 = bf16[24,4608]{1,0:T(8,128)(2,1)S(1)} collective-permute-done((bf16[24,4608]{1,0:T(8,128)(2,1)S(1)}, bf16[24,4608]{1,0:T(8,128)(2,1)S(1)}, u32[]{:S(2)}, u32[]{:S(2)}) %collective-permute-start.21) | collective-permute-done | bytes 221216 | tf_op jit(solution)/shard_map/ppermute | solution.py:24
  123.1 1.8 collective-permute-start.20
  125.0 2.0 %collective-permute-start.22 = (bf16[24,4608]{1,0:T(8,128)(2,1)S(1)}, bf16[24,4608]{1,0:T(8,128)(2,1)S(1)}, u32[]{:S(2)}, u32[]{:S(2)}) collective-permute-start(bf16[24,4608]{1,0:T(8,128)(2,1)S(1)} %add_convert_fusion.2), channel_id=1, source_target_pairs={{0,12},{1,13},{2,14},{3,15},{4,0},{5,1},{6,2},{7,3},{8,4},{9,5},{1... | collective-permute-start | bytes 663560 | tf_op jit(solution)/shard_map/ppermute | solution.py:24
  127.0 3.7 %collective-permute-done.20 = bf16[24,4608]{1,0:T(8,128)(2,1)S(1)} collective-permute-done((bf16[24,4608]{1,0:T(8,128)(2,1)S(1)}, bf16[24,4608]{1,0:T(8,128)(2,1)S(1)}, u32[]{:S(2)}, u32[]{:S(2)}) %collective-permute-start.20) | collective-permute-done | bytes 221216 | tf_op jit(solution)/shard_map/ppermute | solution.py:24
  130.7 4.6 %collective-permute-start.24 = (bf16[96,3584]{1,0:T(8,128)(2,1)S(1)}, bf16[96,3584]{1,0:T(8,128)(2,1)S(1)}, u32[]{:S(2)}, u32[]{:S(2)}) collective-permute-start(bf16[96,3584]{1,0:T(8,128)(2,1)S(1)} %get-tuple-element.36), channel_id=1, source_target_pairs={{0,2},{1,3},{2,0},{3,1},{4,6},{5,7},{6,4},{7,5},{8,10},{9,11},{10,... | collective-permute-start | bytes 2064392 | tf_op jit(solution)/shard_map/ppermute | solution.py:24
  135.5 12.5 %collective-permute-done.24 = bf16[96,3584]{1,0:T(8,128)(2,1)S(1)} collective-permute-done((bf16[96,3584]{1,0:T(8,128)(2,1)S(1)}, bf16[96,3584]{1,0:T(8,128)(2,1)S(1)}, u32[]{:S(2)}, u32[]{:S(2)}) %collective-permute-start.24) | collective-permute-done | bytes 688160 | tf_op jit(solution)/shard_map/ppermute | solution.py:24
  148.0 3.2 %collective-permute-start.23 = (bf16[24,4608]{1,0:T(8,128)(2,1)S(1)}, bf16[24,4608]{1,0:T(8,128)(2,1)S(1)}, u32[]{:S(2)}, u32[]{:S(2)}) collective-permute-start(bf16[24,4608]{1,0:T(8,128)(2,1)S(1)} %add_convert_fusion.1), channel_id=1, source_target_pairs={{0,2},{1,3},{2,0},{3,1},{4,6},{5,7},{6,4},{7,5},{8,10},{9,11},{10,... | collective-permute-start | bytes 663560 | tf_op jit(solution)/shard_map/ppermute | solution.py:24
  151.4 3.2 %collective-permute-start.27 = (bf16[24,3584]{1,0:T(8,128)(2,1)S(1)}, bf16[24,3584]{1,0:T(8,128)(2,1)S(1)}, u32[]{:S(2)}, u32[]{:S(2)}) collective-permute-start(bf16[24,3584]{1,0:T(8,128)(2,1)S(1)} %get-tuple-element.49), channel_id=1, source_target_pairs={{0,8},{1,9},{2,10},{3,11},{4,12},{5,13},{6,14},{7,15},{8,0},{9,1},... | collective-permute-start | bytes 516104 | tf_op jit(solution)/shard_map/ppermute | solution.py:24
  155.4 1.7 collective-permute-start.26
  158.0 2.7 %collective-permute-done.27 = bf16[24,3584]{1,0:T(8,128)(2,1)S(1)} collective-permute-done((bf16[24,3584]{1,0:T(8,128)(2,1)S(1)}, bf16[24,3584]{1,0:T(8,128)(2,1)S(1)}, u32[]{:S(2)}, u32[]{:S(2)}) %collective-permute-start.27) | collective-permute-done | bytes 172064 | tf_op jit(solution)/shard_map/ppermute | solution.py:24
  161.2 1.6 copy_units.6
  162.7 5.5 %all-to-all-start.1 = ((bf16[8,8,8192]{2,1,0:T(8,128)(2,1)}), bf16[8,8,8192]{2,1,0:T(8,128)(2,1)S(1)}, u32[]{:S(2)}, u32[]{:S(2)}) async-start(bf16[8,8,8192]{2,1,0:T(8,128)(2,1)} %bitcast.9), calls=%async_computation.1 | async-start | bytes 2097152 | tf_op jit(solution)/shard_map/all_to_all | solution.py:287
  168.2 2.6 %collective-permute-done.34 = bf16[8,8192]{1,0:T(8,128)(2,1)S(1)} collective-permute-done((bf16[8,8192]{1,0:T(8,128)(2,1)S(1)}, bf16[8,8192]{1,0:T(8,128)(2,1)S(1)}, u32[]{:S(2)}, u32[]{:S(2)}) %collective-permute-start.34) | collective-permute-done | bytes 131104 | tf_op jit(solution)/shard_map/ppermute | solution.py:24
  171.0 8.6 %all-to-all-done.1 = bf16[8,8,8192]{2,1,0:T(8,128)(2,1)S(1)} async-done(((bf16[8,8,8192]{2,1,0:T(8,128)(2,1)}), bf16[8,8,8192]{2,1,0:T(8,128)(2,1)S(1)}, u32[]{:S(2)}, u32[]{:S(2)}) %all-to-all-start.1) | async-done | bytes 1048608 | tf_op jit(solution)/shard_map/all_to_all | solution.py:287
  179.6 1.6 copy_units.7
  (69 shorter events, 8.9 us)
Async XLA Ops:
  0.0 77.2 %copy-start.3 = (s32[4,16]{1,0:T(4,128)S(1)}, s32[4,16]{1,0:T(4,128)}, u32[]{:S(2)}) copy-start(s32[4,16]{1,0:T(4,128)} %param.11) | copy-start | bytes 772
  0.0 77.2 %copy-start.2 = (s32[4,16]{1,0:T(4,128)S(1)}, s32[4,16]{1,0:T(4,128)}, u32[]{:S(2)}) copy-start(s32[4,16]{1,0:T(4,128)} %param.13) | copy-start | bytes 772
  0.0 77.2 %copy-start.1 = (s32[4,16]{1,0:T(4,128)S(1)}, s32[4,16]{1,0:T(4,128)}, u32[]{:S(2)}) copy-start(s32[4,16]{1,0:T(4,128)} %param.15) | copy-start | bytes 772
  0.8 32.4 %collective-permute-start = (s32[3,4,16]{2,1,0:T(4,128)S(1)}, s32[3,4,16]{2,1,0:T(4,128)S(1)}, u32[]{:S(2)}, u32[]{:S(2)}) collective-permute-start(s32[3,4,16]{2,1,0:T(4,128)S(1)} %pad_add_fusion), channel_id=1, source_target_pairs={{0,1},{1,0},{2,3},{3,2},{4,5},{5,4},{6,7},{7,6},{8,9},{9,8},{10,11... | collective-permute-start | bytes 2312 | tf_op jit(solution)/shard_map/ppermute | solution.py:24
  1.7 15.0 %collective-permute-start.13 = (bf16[8,8192]{1,0:T(8,128)(2,1)S(1)}, bf16[8,8192]{1,0:T(8,128)(2,1)S(1)}, u32[]{:S(2)}, u32[]{:S(2)}) collective-permute-start(bf16[8,8192]{1,0:T(8,128)(2,1)S(1)} %slice.39), channel_id=1, source_target_pairs={{0,2},{1,3},{2,0},{3,1},{4,6},{5,7},{6,4},{7,5},{8,10},{9,11},{10,... | collective-permute-start | bytes 393224 | tf_op jit(solution)/shard_map/ppermute | solution.py:24
  8.2 1.2 copy-start
  11.0 21.6 %all-to-all-start = ((bf16[8,8,8192]{2,1,0:T(8,128)(2,1)}), bf16[8,8,8192]{2,1,0:T(8,128)(2,1)S(1)}, u32[]{:S(2)}, u32[]{:S(2)}) async-start(bf16[8,8,8192]{2,1,0:T(8,128)(2,1)} %bitcast.7), calls=%async_computation | async-start | bytes 2097152 | tf_op jit(solution)/shard_map/all_to_all | solution.py:271
  15.9 69.0 %collective-permute-start.1 = (bf16[4,16,128,256]{3,2,1,0:T(8,128)(2,1)}, bf16[4,16,128,256]{3,2,1,0:T(8,128)(2,1)}, u32[]{:S(2)}, u32[]{:S(2)}) collective-permute-start(bf16[4,16,128,256]{3,2,1,0:T(8,128)(2,1)} %gate_own.1), channel_id=1, source_target_pairs={{0,1},{1,0},{2,3},{3,2},{4,5},{5,4},{6,7},{7,6},{8,9},{9,8},{10,11... | collective-permute-start | bytes 12582920 | tf_op jit(solution)/shard_map/ppermute | solution.py:24
  15.9 69.0 %collective-permute-start.2 = (bf16[4,16,128,256]{3,2,1,0:T(8,128)(2,1)}, bf16[4,16,128,256]{3,2,1,0:T(8,128)(2,1)}, u32[]{:S(2)}, u32[]{:S(2)}) collective-permute-start(bf16[4,16,128,256]{3,2,1,0:T(8,128)(2,1)} %up_own.1), channel_id=1, source_target_pairs={{0,1},{1,0},{2,3},{3,2},{4,5},{5,4},{6,7},{7,6},{8,9},{9,8},{10,11... | collective-permute-start | bytes 12582920 | tf_op jit(solution)/shard_map/ppermute | solution.py:24
  16.4 68.5 %collective-permute-start.3 = (bf16[4,16,256,128]{3,2,1,0:T(8,128)(2,1)}, bf16[4,16,256,128]{3,2,1,0:T(8,128)(2,1)}, u32[]{:S(2)}, u32[]{:S(2)}) collective-permute-start(bf16[4,16,256,128]{3,2,1,0:T(8,128)(2,1)} %down_own.1), channel_id=1, source_target_pairs={{0,1},{1,0},{2,3},{3,2},{4,5},{5,4},{6,7},{7,6},{8,9},{9,8},{10,11... | collective-permute-start | bytes 12582920 | tf_op jit(solution)/shard_map/ppermute | solution.py:24
  16.7 17.7 %collective-permute-start.16 = (bf16[16,8192]{1,0:T(8,128)(2,1)S(1)}, bf16[16,8192]{1,0:T(8,128)(2,1)S(1)}, u32[]{:S(2)}, u32[]{:S(2)}) collective-permute-start(bf16[16,8192]{1,0:T(8,128)(2,1)S(1)} %pad_maximum_fusion.rest_8_), channel_id=1, source_target_pairs={{0,8},{1,9},{2,10},{3,11},{4,12},{5,13},{6,14},{7,15},{8,0},{9,1},... | collective-permute-start | bytes 786440 | tf_op jit(solution)/shard_map/ppermute | solution.py:24
  33.2 7.0 %collective-permute-start.4 = (bf16[24,3584]{1,0:T(8,128)(2,1)S(1)}, bf16[24,3584]{1,0:T(8,128)(2,1)S(1)}, u32[]{:S(2)}, u32[]{:S(2)}) collective-permute-start(bf16[24,3584]{1,0:T(8,128)(2,1)S(1)} %get-tuple-element.25), channel_id=1, source_target_pairs={{0,2},{1,3},{2,0},{3,1},{4,6},{5,7},{6,4},{7,5},{8,10},{9,11},{10,... | collective-permute-start | bytes 516104 | tf_op jit(solution)/shard_map/ppermute | solution.py:24
  34.4 7.4 %collective-permute-start.15 = (bf16[16,8192]{1,0:T(8,128)(2,1)S(1)}, bf16[16,8192]{1,0:T(8,128)(2,1)S(1)}, u32[]{:S(2)}, u32[]{:S(2)}) collective-permute-start(bf16[16,8192]{1,0:T(8,128)(2,1)S(1)} %pad_maximum_fusion.rest_8_), channel_id=1, source_target_pairs={{0,12},{1,13},{2,14},{3,15},{4,0},{5,1},{6,2},{7,3},{8,4},{9,5},{1... | collective-permute-start | bytes 786440 | tf_op jit(solution)/shard_map/ppermute | solution.py:24
  40.2 9.4 %collective-permute-start.8 = (bf16[24,4608]{1,0:T(8,128)(2,1)S(1)}, bf16[24,4608]{1,0:T(8,128)(2,1)S(1)}, u32[]{:S(2)}, u32[]{:S(2)}) collective-permute-start(bf16[24,4608]{1,0:T(8,128)(2,1)S(1)} %get-tuple-element.26.rest_4_), channel_id=1, source_target_pairs={{0,4},{1,5},{2,6},{3,7},{4,8},{5,9},{6,10},{7,11},{8,12},{9,13},{1... | collective-permute-start | bytes 663560 | tf_op jit(solution)/shard_map/ppermute | solution.py:24
  41.8 10.5 %collective-permute-start.14 = (bf16[16,8192]{1,0:T(8,128)(2,1)S(1)}, bf16[16,8192]{1,0:T(8,128)(2,1)S(1)}, u32[]{:S(2)}, u32[]{:S(2)}) collective-permute-start(bf16[16,8192]{1,0:T(8,128)(2,1)S(1)} %pad_maximum_fusion.rest_8_), channel_id=1, source_target_pairs={{0,4},{1,5},{2,6},{3,7},{4,8},{5,9},{6,10},{7,11},{8,12},{9,13},{1... | collective-permute-start | bytes 786440 | tf_op jit(solution)/shard_map/ppermute | solution.py:24
  49.5 6.0 %collective-permute-start.9 = (bf16[24,4608]{1,0:T(8,128)(2,1)S(1)}, bf16[24,4608]{1,0:T(8,128)(2,1)S(1)}, u32[]{:S(2)}, u32[]{:S(2)}) collective-permute-start(bf16[24,4608]{1,0:T(8,128)(2,1)S(1)} %get-tuple-element.26.rest_4_), channel_id=1, source_target_pairs={{0,12},{1,13},{2,14},{3,15},{4,0},{5,1},{6,2},{7,3},{8,4},{9,5},{1... | collective-permute-start | bytes 663560 | tf_op jit(solution)/shard_map/ppermute | solution.py:24
  52.3 7.4 %collective-permute-start.11 = (bf16[24,4608]{1,0:T(8,128)(2,1)S(1)}, bf16[24,4608]{1,0:T(8,128)(2,1)S(1)}, u32[]{:S(2)}, u32[]{:S(2)}) collective-permute-start(bf16[24,4608]{1,0:T(8,128)(2,1)S(1)} %get-tuple-element.26.rest_4_), channel_id=1, source_target_pairs={{0,2},{1,3},{2,0},{3,1},{4,6},{5,7},{6,4},{7,5},{8,10},{9,11},{10,... | collective-permute-start | bytes 663560 | tf_op jit(solution)/shard_map/ppermute | solution.py:24
  55.6 9.8 %collective-permute-start.10 = (bf16[24,4608]{1,0:T(8,128)(2,1)S(1)}, bf16[24,4608]{1,0:T(8,128)(2,1)S(1)}, u32[]{:S(2)}, u32[]{:S(2)}) collective-permute-start(bf16[24,4608]{1,0:T(8,128)(2,1)S(1)} %get-tuple-element.26.rest_4_), channel_id=1, source_target_pairs={{0,8},{1,9},{2,10},{3,11},{4,12},{5,13},{6,14},{7,15},{8,0},{9,1},... | collective-permute-start | bytes 663560 | tf_op jit(solution)/shard_map/ppermute | solution.py:24
  59.8 10.8 %collective-permute-start.7 = (bf16[48,3584]{1,0:T(8,128)(2,1)S(1)}, bf16[48,3584]{1,0:T(8,128)(2,1)S(1)}, u32[]{:S(2)}, u32[]{:S(2)}) collective-permute-start(bf16[48,3584]{1,0:T(8,128)(2,1)S(1)} %constant_dynamic-update-slice_fusion.rest_0_), channel_id=1, source_target_pairs={{0,8},{1,9},{2,10},{3,11},{4,12},{5,13},{6,14},{7,15},{8,0},{9,1},... | collective-permute-start | bytes 1032200 | tf_op jit(solution)/shard_map/ppermute | solution.py:24
  65.4 10.9 %collective-permute-start.6 = (bf16[48,3584]{1,0:T(8,128)(2,1)S(1)}, bf16[48,3584]{1,0:T(8,128)(2,1)S(1)}, u32[]{:S(2)}, u32[]{:S(2)}) collective-permute-start(bf16[48,3584]{1,0:T(8,128)(2,1)S(1)} %constant_dynamic-update-slice_fusion.rest_0_), channel_id=1, source_target_pairs={{0,12},{1,13},{2,14},{3,15},{4,0},{5,1},{6,2},{7,3},{8,4},{9,5},{1... | collective-permute-start | bytes 1032200 | tf_op jit(solution)/shard_map/ppermute | solution.py:24
  70.6 14.4 %collective-permute-start.12 = (bf16[72,4608]{1,0:T(8,128)(2,1)S(1)}, bf16[72,4608]{1,0:T(8,128)(2,1)S(1)}, u32[]{:S(2)}, u32[]{:S(2)}) collective-permute-start(bf16[72,4608]{1,0:T(8,128)(2,1)S(1)} %constant_dynamic-update-slice_fusion.2.rest_5_), channel_id=1, source_target_pairs={{0,2},{1,3},{2,0},{3,1},{4,6},{5,7},{6,4},{7,5},{8,10},{9,11},{10,... | collective-permute-start | bytes 1990664 | tf_op jit(solution)/shard_map/ppermute | solution.py:24
  76.3 8.5 %collective-permute-start.5 = (bf16[48,3584]{1,0:T(8,128)(2,1)S(1)}, bf16[48,3584]{1,0:T(8,128)(2,1)S(1)}, u32[]{:S(2)}, u32[]{:S(2)}) collective-permute-start(bf16[48,3584]{1,0:T(8,128)(2,1)S(1)} %constant_dynamic-update-slice_fusion.rest_0_), channel_id=1, source_target_pairs={{0,4},{1,5},{2,6},{3,7},{4,8},{5,9},{6,10},{7,11},{8,12},{9,13},{1... | collective-permute-start | bytes 1032200 | tf_op jit(solution)/shard_map/ppermute | solution.py:24
  103.8 9.3 %collective-permute-start.31 = (bf16[8,8192]{1,0:T(8,128)(2,1)S(1)}, bf16[8,8192]{1,0:T(8,128)(2,1)S(1)}, u32[]{:S(2)}, u32[]{:S(2)}) collective-permute-start(bf16[8,8192]{1,0:T(8,128)(2,1)S(1)} %get-tuple-element.42), channel_id=1, source_target_pairs={{0,4},{1,5},{2,6},{3,7},{4,8},{5,9},{6,10},{7,11},{8,12},{9,13},{1... | collective-permute-start | bytes 393224 | tf_op jit(solution)/shard_map/ppermute | solution.py:24
  104.8 8.6 %collective-permute-start.32 = (bf16[8,8192]{1,0:T(8,128)(2,1)S(1)}, bf16[8,8192]{1,0:T(8,128)(2,1)S(1)}, u32[]{:S(2)}, u32[]{:S(2)}) collective-permute-start(bf16[8,8192]{1,0:T(8,128)(2,1)S(1)} %get-tuple-element.43), channel_id=1, source_target_pairs={{0,12},{1,13},{2,14},{3,15},{4,0},{5,1},{6,2},{7,3},{8,4},{9,5},{1... | collective-permute-start | bytes 393224 | tf_op jit(solution)/shard_map/ppermute | solution.py:24
  107.1 9.3 %collective-permute-start.33 = (bf16[8,8192]{1,0:T(8,128)(2,1)S(1)}, bf16[8,8192]{1,0:T(8,128)(2,1)S(1)}, u32[]{:S(2)}, u32[]{:S(2)}) collective-permute-start(bf16[8,8192]{1,0:T(8,128)(2,1)S(1)} %get-tuple-element.44), channel_id=1, source_target_pairs={{0,8},{1,9},{2,10},{3,11},{4,12},{5,13},{6,14},{7,15},{8,0},{9,1},... | collective-permute-start | bytes 393224 | tf_op jit(solution)/shard_map/ppermute | solution.py:24
  109.9 58.3 %collective-permute-start.28 = (bf16[8,8192]{1,0:T(8,128)(2,1)S(1)}, bf16[8,8192]{1,0:T(8,128)(2,1)S(1)}, u32[]{:S(2)}, u32[]{:S(2)}) collective-permute-start(bf16[8,8192]{1,0:T(8,128)(2,1)S(1)} %get-tuple-element.38), channel_id=1, source_target_pairs={{0,4},{1,5},{2,6},{3,7},{4,8},{5,9},{6,10},{7,11},{8,12},{9,13},{1... | collective-permute-start | bytes 393224 | tf_op jit(solution)/shard_map/ppermute | solution.py:24
  111.3 56.9 %collective-permute-start.29 = (bf16[8,8192]{1,0:T(8,128)(2,1)S(1)}, bf16[8,8192]{1,0:T(8,128)(2,1)S(1)}, u32[]{:S(2)}, u32[]{:S(2)}) collective-permute-start(bf16[8,8192]{1,0:T(8,128)(2,1)S(1)} %get-tuple-element.39), channel_id=1, source_target_pairs={{0,12},{1,13},{2,14},{3,15},{4,0},{5,1},{6,2},{7,3},{8,4},{9,5},{1... | collective-permute-start | bytes 393224 | tf_op jit(solution)/shard_map/ppermute | solution.py:24
  113.1 11.9 %collective-permute-start.17 = (bf16[24,4608]{1,0:T(8,128)(2,1)S(1)}, bf16[24,4608]{1,0:T(8,128)(2,1)S(1)}, u32[]{:S(2)}, u32[]{:S(2)}) collective-permute-start(bf16[24,4608]{1,0:T(8,128)(2,1)S(1)} %get-tuple-element.29), channel_id=1, source_target_pairs={{0,4},{1,5},{2,6},{3,7},{4,8},{5,9},{6,10},{7,11},{8,12},{9,13},{1... | collective-permute-start | bytes 663560 | tf_op jit(solution)/shard_map/ppermute | solution.py:24
  113.4 38.0 %collective-permute-start.19 = (bf16[24,4608]{1,0:T(8,128)(2,1)S(1)}, bf16[24,4608]{1,0:T(8,128)(2,1)S(1)}, u32[]{:S(2)}, u32[]{:S(2)}) collective-permute-start(bf16[24,4608]{1,0:T(8,128)(2,1)S(1)} %get-tuple-element.30), channel_id=1, source_target_pairs={{0,12},{1,13},{2,14},{3,15},{4,0},{5,1},{6,2},{7,3},{8,4},{9,5},{1... | collective-permute-start | bytes 663560 | tf_op jit(solution)/shard_map/ppermute | solution.py:24
  116.4 6.8 %collective-permute-start.21 = (bf16[24,4608]{1,0:T(8,128)(2,1)S(1)}, bf16[24,4608]{1,0:T(8,128)(2,1)S(1)}, u32[]{:S(2)}, u32[]{:S(2)}) collective-permute-start(bf16[24,4608]{1,0:T(8,128)(2,1)S(1)} %get-tuple-element.34), channel_id=1, source_target_pairs={{0,12},{1,13},{2,14},{3,15},{4,0},{5,1},{6,2},{7,3},{8,4},{9,5},{1... | collective-permute-start | bytes 663560 | tf_op jit(solution)/shard_map/ppermute | solution.py:24
  123.1 7.6 %collective-permute-start.20 = (bf16[24,4608]{1,0:T(8,128)(2,1)S(1)}, bf16[24,4608]{1,0:T(8,128)(2,1)S(1)}, u32[]{:S(2)}, u32[]{:S(2)}) collective-permute-start(bf16[24,4608]{1,0:T(8,128)(2,1)S(1)} %get-tuple-element.32), channel_id=1, source_target_pairs={{0,4},{1,5},{2,6},{3,7},{4,8},{5,9},{6,10},{7,11},{8,12},{9,13},{1... | collective-permute-start | bytes 663560 | tf_op jit(solution)/shard_map/ppermute | solution.py:24
  125.0 10.3 %collective-permute-start.22 = (bf16[24,4608]{1,0:T(8,128)(2,1)S(1)}, bf16[24,4608]{1,0:T(8,128)(2,1)S(1)}, u32[]{:S(2)}, u32[]{:S(2)}) collective-permute-start(bf16[24,4608]{1,0:T(8,128)(2,1)S(1)} %add_convert_fusion.2), channel_id=1, source_target_pairs={{0,12},{1,13},{2,14},{3,15},{4,0},{5,1},{6,2},{7,3},{8,4},{9,5},{1... | collective-permute-start | bytes 663560 | tf_op jit(solution)/shard_map/ppermute | solution.py:24
  130.7 17.2 %collective-permute-start.24 = (bf16[96,3584]{1,0:T(8,128)(2,1)S(1)}, bf16[96,3584]{1,0:T(8,128)(2,1)S(1)}, u32[]{:S(2)}, u32[]{:S(2)}) collective-permute-start(bf16[96,3584]{1,0:T(8,128)(2,1)S(1)} %get-tuple-element.36), channel_id=1, source_target_pairs={{0,2},{1,3},{2,0},{3,1},{4,6},{5,7},{6,4},{7,5},{8,10},{9,11},{10,... | collective-permute-start | bytes 2064392 | tf_op jit(solution)/shard_map/ppermute | solution.py:24
  135.4 16.1 %collective-permute-start.18 = (bf16[24,4608]{1,0:T(8,128)(2,1)S(1)}, bf16[24,4608]{1,0:T(8,128)(2,1)S(1)}, u32[]{:S(2)}, u32[]{:S(2)}) collective-permute-start(bf16[24,4608]{1,0:T(8,128)(2,1)S(1)} %add_convert_fusion.3), channel_id=1, source_target_pairs={{0,4},{1,5},{2,6},{3,7},{4,8},{5,9},{6,10},{7,11},{8,12},{9,13},{1... | collective-permute-start | bytes 663560 | tf_op jit(solution)/shard_map/ppermute | solution.py:24
  148.0 7.4 %collective-permute-start.23 = (bf16[24,4608]{1,0:T(8,128)(2,1)S(1)}, bf16[24,4608]{1,0:T(8,128)(2,1)S(1)}, u32[]{:S(2)}, u32[]{:S(2)}) collective-permute-start(bf16[24,4608]{1,0:T(8,128)(2,1)S(1)} %add_convert_fusion.1), channel_id=1, source_target_pairs={{0,2},{1,3},{2,0},{3,1},{4,6},{5,7},{6,4},{7,5},{8,10},{9,11},{10,... | collective-permute-start | bytes 663560 | tf_op jit(solution)/shard_map/ppermute | solution.py:24
  151.4 6.7 %collective-permute-start.25 = (bf16[24,3584]{1,0:T(8,128)(2,1)S(1)}, bf16[24,3584]{1,0:T(8,128)(2,1)S(1)}, u32[]{:S(2)}, u32[]{:S(2)}) collective-permute-start(bf16[24,3584]{1,0:T(8,128)(2,1)S(1)} %get-tuple-element.48), channel_id=1, source_target_pairs={{0,4},{1,5},{2,6},{3,7},{4,8},{5,9},{6,10},{7,11},{8,12},{9,13},{1... | collective-permute-start | bytes 516104 | tf_op jit(solution)/shard_map/ppermute | solution.py:24
  151.4 9.3 %collective-permute-start.27 = (bf16[24,3584]{1,0:T(8,128)(2,1)S(1)}, bf16[24,3584]{1,0:T(8,128)(2,1)S(1)}, u32[]{:S(2)}, u32[]{:S(2)}) collective-permute-start(bf16[24,3584]{1,0:T(8,128)(2,1)S(1)} %get-tuple-element.49), channel_id=1, source_target_pairs={{0,8},{1,9},{2,10},{3,11},{4,12},{5,13},{6,14},{7,15},{8,0},{9,1},... | collective-permute-start | bytes 516104 | tf_op jit(solution)/shard_map/ppermute | solution.py:24
  155.4 5.6 %collective-permute-start.26 = (bf16[24,3584]{1,0:T(8,128)(2,1)S(1)}, bf16[24,3584]{1,0:T(8,128)(2,1)S(1)}, u32[]{:S(2)}, u32[]{:S(2)}) collective-permute-start(bf16[24,3584]{1,0:T(8,128)(2,1)S(1)} %get-tuple-element.50), channel_id=1, source_target_pairs={{0,12},{1,13},{2,14},{3,15},{4,0},{5,1},{6,2},{7,3},{8,4},{9,5},{1... | collective-permute-start | bytes 516104 | tf_op jit(solution)/shard_map/ppermute | solution.py:24
  158.0 10.2 %collective-permute-start.30 = (bf16[8,8192]{1,0:T(8,128)(2,1)S(1)}, bf16[8,8192]{1,0:T(8,128)(2,1)S(1)}, u32[]{:S(2)}, u32[]{:S(2)}) collective-permute-start(bf16[8,8192]{1,0:T(8,128)(2,1)S(1)} %get-tuple-element.40), channel_id=1, source_target_pairs={{0,8},{1,9},{2,10},{3,11},{4,12},{5,13},{6,14},{7,15},{8,0},{9,1},... | collective-permute-start | bytes 393224 | tf_op jit(solution)/shard_map/ppermute | solution.py:24
  160.8 10.1 %collective-permute-start.34 = (bf16[8,8192]{1,0:T(8,128)(2,1)S(1)}, bf16[8,8192]{1,0:T(8,128)(2,1)S(1)}, u32[]{:S(2)}, u32[]{:S(2)}) collective-permute-start(bf16[8,8192]{1,0:T(8,128)(2,1)S(1)} %add_convert_fusion.9), channel_id=1, source_target_pairs={{0,2},{1,3},{2,0},{3,1},{4,6},{5,7},{6,4},{7,5},{8,10},{9,11},{10,... | collective-permute-start | bytes 393224 | tf_op jit(solution)/shard_map/ppermute | solution.py:24
  162.7 16.9 %all-to-all-start.1 = ((bf16[8,8,8192]{2,1,0:T(8,128)(2,1)}), bf16[8,8,8192]{2,1,0:T(8,128)(2,1)S(1)}, u32[]{:S(2)}, u32[]{:S(2)}) async-start(bf16[8,8,8192]{2,1,0:T(8,128)(2,1)} %bitcast.9), calls=%async_computation.1 | async-start | bytes 2097152 | tf_op jit(solution)/shard_map/all_to_all | solution.py:287
